TPU v7x, 1024 devices: a whole 4x8x16 slice. The times are simulated.
1024 devices in a mesh: dp: 16 (over y, core), ep: 64 (over x, z).
Axes of the slice: x: 4, y: 8, z: 16, core: 2. Of those that a mesh axis runs over, the one named last changes fastest.
Arguments:
- expert_ids: int32 [16, 1024, 8], P('dp', 'ep'), may hold values from 0 to 63, all different within a row; in each aligned block of 16 rows (0 to 15, 16 to 31, ..., all dimensions but the last counted through in order) at most 4 rows name the same one
- route_weights: float32 [16, 1024, 8], P('dp', 'ep'), may hold values from 0.03 to 0.4
- saved_rows: bfloat16 [16, 64, 256, 2048], P('dp', 'ep'), may hold values from -6 to 6
- saved_gate_up: bfloat16 [16, 64, 256, 1536], P('dp', 'ep'), may hold values from -6 to 6
- hidden_grad: bfloat16 [16, 64, 256, 768], P('dp', 'ep'), may hold values from -6 to 6
- gate_up_weight: bfloat16 [64, 2048, 1536], P('ep'), may hold values from -0.125 to 0.125
Outputs:
- input_grad: bfloat16 [16, 1024, 2048], P('dp', 'ep')
- weight_grad: float32 [2048, 64, 1536], P('dp', 'ep')
Inputs may be any that keep to these rules, and one draw needn't show every extreme that they name: `expert_ids`: each token names 8 different experts; among the tokens of one device no expert is named more than 4 times, a bound that some block reaches.
All inputs are finite; a program needn't handle non-finite values.
Results may differ from a plain program's by a relative error of at most 0.017.
Values may be sent and summed in bfloat16 or wider, within the bound.
No kernel may reach another device: no remote copies, remote signals or barrier semaphores. Data moves between devices by JAX's collectives and lax.ppermute only.
A program may use at most 64 MiB of HBM per device.

v0:
```python
import jax
import jax.numpy as jnp
from jax import lax
from jax.sharding import PartitionSpec as P


def shards(expert_ids, route_weights, saved_rows, saved_gate_up, hidden_grad, gate_up_weight):
    tokens_here = expert_ids.shape[1]
    chosen = expert_ids.shape[2]
    model_width = saved_rows.shape[3]
    slot_total = saved_rows.shape[2]
    hidden_units = hidden_grad.shape[3]
    experts = lax.axis_size("ep")
    replicas = lax.axis_size("dp")
    capacity = slot_total // experts
    flat_ids = expert_ids.reshape(tokens_here * chosen)
    onehot = (flat_ids[:, None] == jnp.arange(experts, dtype=jnp.int32)[None, :]).astype(jnp.int32)
    before = jnp.cumsum(onehot, axis=0) - onehot
    rank_in_block = jnp.sum(before * onehot, axis=1)
    counts = jnp.sum(onehot, axis=0)
    sources = lax.all_to_all(
        counts.reshape(experts, 1), "ep", split_axis=0, concat_axis=0, tiled=True
    )
    live_mask = (jnp.arange(capacity, dtype=jnp.int32)[None, :] < sources).reshape(
        1, 1, slot_total, 1
    )
    gate_pre = saved_gate_up[..., :hidden_units].astype(jnp.float32)
    up_pre = saved_gate_up[..., hidden_units:].astype(jnp.float32)
    grad_hidden = hidden_grad.astype(jnp.float32)
    sigma_gate = jax.nn.sigmoid(gate_pre)
    grad_gate = grad_hidden * up_pre * sigma_gate * (1.0 + gate_pre * (1.0 - sigma_gate))
    grad_up = grad_hidden * gate_pre * sigma_gate
    slot_grads = (
        jnp.concatenate([grad_gate, grad_up], axis=-1) * live_mask.astype(jnp.float32)
    ).astype(jnp.bfloat16)
    grads_flat = slot_grads.reshape(slot_total, 2 * hidden_units)
    rows_flat = saved_rows.reshape(slot_total, model_width)
    share = model_width // replicas
    product = lax.dot_general(
        rows_flat, grads_flat, (((0,), (0,)), ((), ())), preferred_element_type=jnp.float32
    )
    summed = lax.psum_scatter(
        product.reshape(share * lax.axis_size("dp"), 1, 2 * hidden_units).astype(jnp.bfloat16),
        "dp",
        scatter_dimension=0,
        tiled=True,
    ).astype(jnp.float32)
    weight_grad = summed / replicas
    weight_flat = gate_up_weight.reshape(model_width, 2 * hidden_units)
    row_grads = lax.dot_general(
        grads_flat, weight_flat, (((1,), (1,)), ((), ())), preferred_element_type=jnp.float32
    )
    row_grads = row_grads.astype(jnp.bfloat16).reshape(experts, capacity, model_width)
    returned = lax.all_to_all(row_grads, "ep", split_axis=0, concat_axis=0, tiled=True)
    flat_rows = returned.reshape(experts * capacity, model_width)
    picked = flat_rows[flat_ids * capacity + rank_in_block]
    combined = jnp.sum(
        route_weights.reshape(tokens_here, chosen, 1)
        * picked.reshape(tokens_here, chosen, model_width).astype(jnp.float32),
        axis=1,
    )
    input_grad = combined.astype(jnp.bfloat16).reshape(1, tokens_here, model_width)
    return (input_grad, weight_grad)


def solution(mesh):
    in_specs = (
        P("dp", "ep", None),
        P("dp", "ep", None),
        P("dp", "ep", None, None),
        P("dp", "ep", None, None),
        P("dp", "ep", None, None),
        P("ep", None, None),
    )
    out_specs = (P("dp", "ep", None), P("dp", "ep", None))
    return jax.shard_map(shards, mesh=mesh, in_specs=in_specs, out_specs=out_specs, check_vma=False)
```

profile of v0, /device:TPU:8, one launch (start us, length us, event | category | flops | bytes accessed | tf_op | source)
XLA Modules:
  0.0 138.3 jit_solution(11459583322633008360)
XLA Ops:
  7.2 0.0 copy-start
  7.2 0.8 copy.22
  8.0 0.1 eq.15
  8.1 0.1 fusion.19
  8.2 0.2 reduce_window_sum.11
  8.4 0.2 select_reduce_fusion
  8.6 0.7 copy.23
  9.3 22.2 %all-to-all-start = ((s32[64,1,1]{2,1,0:T(1,128)}), s32[64,1,1]{2,1,0:T(1,128)S(1)}, u32[]{:S(2)}, u32[]{:S(2)}) async-start(s32[64,1,1]{2,1,0:T(1,128)} %copy.23), calls=%async_computation | async-start | bytes 65536 | tf_op jit(solution)/shard_map/all_to_all | solution.py:21
  31.5 0.0 reduce-scatter.4.cloned.1.call-start
  31.6 1.6 %fusion.11 = (f32[1,1,256,1,1,1,1,768]{7,2,6,5,4,3,1,0:T(8,128)S(1)}, f32[1,1,256,1,1,1,1,768]{7,2,6,5,4,3,1,0:T(8,128)S(1)}) fusion(bf16[1,1,256,768]{3,2,1,0:T(8,128)(2,1)} %param.10, bf16[1,1,256,1536]{3,2,1,0:T(8,128)(2,1)} %param.9), kind=kLoop, calls=%fused_computation.17 | loop fusion | flops 2752512 | bytes 2752512 | tf_op jit(solution)/shard_map/concatenate | solution.py:34
  33.2 12.7 %all-to-all-done = s32[64,1,1]{2,1,0:T(1,128)S(1)} async-done(((s32[64,1,1]{2,1,0:T(1,128)}), s32[64,1,1]{2,1,0:T(1,128)S(1)}, u32[]{:S(2)}, u32[]{:S(2)}) %all-to-all-start) | async-done | bytes 288 | tf_op jit(solution)/shard_map/all_to_all | solution.py:21
  45.9 1.2 reduce
  47.1 0.1 fusion.21
  47.2 0.1 reshape.204
  47.3 0.0 copy-done
  47.3 4.6 %fusion = bf16[2048,1536]{0,1:T(8,128)(2,1)} fusion(bf16[1,1,256,2048]{3,2,1,0:T(8,128)(2,1)S(1)} %copy-done, f32[1,1,256,1,1,1,1,768]{7,2,6,5,4,3,1,0:T(8,128)S(1)} %get-tuple-element.13, f32[1,1,256,1,1,1,1,768]{7,2,6,5,4,3,1,0:T(8,128)S(1)} %get-tuple-element.12, f32[256]{0:T(256)S(1)} %reshape.204), kind=kOutput, calls=%fused_computation.2 | convolution fusion | flops 1614938112 | bytes 8913920 | tf_op jit(solution)/shard_map/dot_general | solution.py:39
  51.9 8.7 %copy.28 = bf16[2048,1536]{1,0:T(8,128)(2,1)} copy(bf16[2048,1536]{0,1:T(8,128)(2,1)} %fusion) | data formatting | bytes 12582912
  60.6 0.0 reduce-scatter.4.cloned.1.call-update
  60.6 5.6 %fusion.3 = bf16[256,2048]{1,0:T(8,128)(2,1)} fusion(bf16[1,2048,1536]{2,1,0:T(8,128)(2,1)} %param.11, f32[1,1,256,1,1,1,1,768]{7,2,6,5,4,3,1,0:T(8,128)S(1)} %get-tuple-element.13, f32[1,1,256,1,1,1,1,768]{7,2,6,5,4,3,1,0:T(8,128)S(1)} %get-tuple-element.12, f32[256]{0:T(256)S(1)} %reshape.204), kind=kOutput, calls=%fused_computation.5 | convolution fusion | flops 1612316672 | bytes 8913920 | tf_op jit(solution)/shard_map/dot_general | solution.py:50
  66.3 2.3 %reshape.201 = bf16[64,4,2048]{2,1,0:T(4,128)(2,1)} reshape(bf16[256,2048]{1,0:T(8,128)(2,1)} %fusion.3) | data formatting | bytes 2097152 | tf_op jit(solution)/shard_map/reshape | solution.py:53
  68.5 0.0 copy-start.1
  68.5 0.0 copy-start.2
  68.5 4.8 %all-to-all-start.1 = ((bf16[64,4,2048]{2,1,0:T(4,128)(2,1)}), bf16[64,4,2048]{2,1,0:T(4,128)(2,1)S(1)}, u32[]{:S(2)}, u32[]{:S(2)}) async-start(bf16[64,4,2048]{2,1,0:T(4,128)(2,1)} %reshape.201), calls=%async_computation.1 | async-start | bytes 2097152 | tf_op jit(solution)/shard_map/all_to_all | solution.py:54
  73.3 0.0 copy-done.1
  73.3 0.1 copy.24
  73.4 0.1 mul.87
  73.5 0.0 copy-done.2
  73.5 0.1 copy.21
  73.6 52.5 %all-to-all-done.1 = bf16[64,4,2048]{2,1,0:T(4,128)(2,1)S(1)} async-done(((bf16[64,4,2048]{2,1,0:T(4,128)(2,1)}), bf16[64,4,2048]{2,1,0:T(4,128)(2,1)S(1)}, u32[]{:S(2)}, u32[]{:S(2)}) %all-to-all-start.1) | async-done | bytes 1048608 | tf_op jit(solution)/shard_map/all_to_all | solution.py:54
  126.1 0.3 reshape.202
  126.4 0.9 gather_fusion
  127.3 1.1 fusion.7
  128.4 0.0 reduce-scatter.4.cloned.1.call-done
  128.4 1.2 copy.29
  129.6 0.1 convert_multiply_fusion.4
  129.7 1.7 %copy.25 = f32[128,1,1536]{2,1,0:T(1,128)} copy(f32[128,1,1536]{0,2,1:T(8,128)S(1)} %convert_multiply_fusion.4) | data formatting | bytes 1572864
  (3 shorter events, 0.0 us)
Async XLA Ops:
  7.2 40.1 %copy-start = (bf16[1,1,256,2048]{3,2,1,0:T(8,128)(2,1)S(1)}, bf16[1,1,256,2048]{3,2,1,0:T(8,128)(2,1)}, u32[]{:S(2)}) copy-start(bf16[1,1,256,2048]{3,2,1,0:T(8,128)(2,1)} %param.8) | copy-start | bytes 3145732
  9.3 36.6 %all-to-all-start = ((s32[64,1,1]{2,1,0:T(1,128)}), s32[64,1,1]{2,1,0:T(1,128)S(1)}, u32[]{:S(2)}, u32[]{:S(2)}) async-start(s32[64,1,1]{2,1,0:T(1,128)} %copy.23), calls=%async_computation | async-start | bytes 65536 | tf_op jit(solution)/shard_map/all_to_all | solution.py:21
  31.5 96.9 %reduce-scatter.4.cloned.1.call-start = ((), (), s32[]{:S(2)}) async-start(), calls=%async_computation.3 | async-start | bytes 6684672
  68.5 4.8 %copy-start.1 = (s32[1,16,8]{1,2,0:T(8,128)S(1)}, s32[1,16,8]{1,2,0:T(8,128)}, u32[]{:S(2)}) copy-start(s32[1,16,8]{1,2,0:T(8,128)} %param.6) | copy-start | bytes 1540
  68.5 5.0 %copy-start.2 = (f32[1,16,8]{1,2,0:T(8,128)S(1)}, f32[1,16,8]{1,2,0:T(8,128)}, u32[]{:S(2)}) copy-start(f32[1,16,8]{1,2,0:T(8,128)} %param.7) | copy-start | bytes 1540
  68.5 57.6 %all-to-all-start.1 = ((bf16[64,4,2048]{2,1,0:T(4,128)(2,1)}), bf16[64,4,2048]{2,1,0:T(4,128)(2,1)S(1)}, u32[]{:S(2)}, u32[]{:S(2)}) async-start(bf16[64,4,2048]{2,1,0:T(4,128)(2,1)} %reshape.201), calls=%async_computation.1 | async-start | bytes 2097152 | tf_op jit(solution)/shard_map/all_to_all | solution.py:54
Sparse Core Ops, SparseCore 0:
  60.7 61.8 reduce-scatter.3
where the time goes:
time: 139 us; the launch traced here: 138 us
  waiting for transfers between devices  65.3 us (47%)
  starting transfers between devices  27.1 us (19%)
  local copies, waits for them, and re-layouts  17.1 us (12%)
  between operations  14.1 us (10%)
  matrix products  10.2 us (7%)
  other arithmetic  4.51 us (3%)
    all_to_all x1, waiting for transfers between devices, shards(): lax.all_to_all(row_grads, 'ep', split_axis=0, concat_axis=0, tiled=True)  52.5 us
    all_to_all x1, starting transfers between devices, shards(): lax.all_to_all(counts.reshape(experts, 1), 'ep', split_axis=0, concat_axi...  22.2 us
    all_to_all x1, waiting for transfers between devices, shards(): lax.all_to_all(counts.reshape(experts, 1), 'ep', split_axis=0, concat_axi...  12.7 us
    unnamed x10, local copies, waits for them, and re-layouts  12.5 us
    dot_general x1, matrix products, shards(): lax.dot_general(grads_flat, weight_flat, (((1,), (1,)), ((), ())), prefer...  5.63 us
    all_to_all x1, starting transfers between devices, shards(): lax.all_to_all(row_grads, 'ep', split_axis=0, concat_axis=0, tiled=True)  4.78 us
    dot_general x1, matrix products, shards(): lax.dot_general(rows_flat, grads_flat, (((0,), (0,)), ((), ())), preferre...  4.6 us
  transfers between devices with their start and end apart: 3, of which 2 were waited for; matrix products, arithmetic and copies ran while one was open for 9% of the time, Pallas kernels for 0%

commit v1 on v0

v1 whole, which is shorter than its diff:
```python
import functools
import jax
import jax.numpy as jnp
from jax import lax
from jax.experimental import pallas as pl
from jax.experimental.pallas import tpu as pltpu
from jax.sharding import PartitionSpec as P

ROWS_LIMIT = 60 << 20
BF16, F32, I32 = jnp.bfloat16, jnp.float32, jnp.int32


def dot(a, b, ca, cb):
    return lax.dot_general(a, b, (((ca,), (cb,)), ((), ())), preferred_element_type=F32)


def iota(shape, dim):
    return lax.broadcasted_iota(I32, shape, dim)


def cost(flops, nbytes):
    return pl.CostEstimate(flops=flops, bytes_accessed=nbytes, transcendentals=0)


def flatten_pairs(x_t):
    chosen, tokens = x_t.shape
    pairs = chosen * tokens
    pair = iota((chosen, pairs), 1)
    mine = pair % chosen == iota((chosen, pairs), 0)
    out = jnp.zeros((chosen, pairs), x_t.dtype)
    for t in range(tokens):
        out = jnp.where(mine & (pair // chosen == t), x_t[:, t : t + 1], out)
    return jnp.sum(out, axis=0, keepdims=True)


def route_kernel(ids_ref, cnt_ref, tgt_ref):
    experts = cnt_ref.shape[0]
    flat = flatten_pairs(ids_ref[...])
    pairs = flat.shape[1]
    onehot = (iota((experts, pairs), 0) == flat).astype(F32)
    upper = (iota((pairs, pairs), 0) < iota((pairs, pairs), 1)).astype(BF16)
    before = dot(onehot.astype(BF16), upper, 1, 0)
    rank = jnp.sum(before * onehot, axis=0, keepdims=True).astype(I32)
    tgt_ref[...] = flat * 8 + rank
    counts = jnp.sum(onehot, axis=1, keepdims=True).astype(I32)
    cnt_ref[:, 0, :] = jnp.broadcast_to(counts, (experts, cnt_ref.shape[2]))


def rows_kernel(me_ref, gu_ref, hg_ref, rows_ref, wlo_ref, whi_ref, trade_ref, out_ref, grads_ref):
    @pl.when(pl.program_id(0) == 0)
    def _():
        hidden = hg_ref.shape[1]
        gate = gu_ref[:, :hidden].astype(F32)
        up = gu_ref[:, hidden:].astype(F32)
        grad = hg_ref[...].astype(F32)
        sigma = jax.nn.sigmoid(gate)
        grads_ref[:, :hidden] = (grad * up * sigma * (1.0 + gate * (1.0 - sigma))).astype(BF16)
        grads_ref[:, hidden:] = (grad * gate * sigma).astype(BF16)
        part = trade_ref.shape[2]
        tiles = 2 * hidden // part
        for tile in range(tiles):
            trade_ref[tile] = grads_ref[:, tile * part : (tile + 1) * part]
        second = lax.rem(me_ref[0], 2) == 0
        for chunk in range(trade_ref.shape[0] - tiles):
            start = 2 * chunk * part
            trade_ref[tiles + chunk] = jnp.where(
                second,
                rows_ref[:, start + part : start + 2 * part],
                rows_ref[:, start : start + part],
            )

    grads = grads_ref[...]
    low = dot(grads, wlo_ref[...], 1, 1)
    high = dot(grads, whi_ref[...], 1, 1)
    slots, width = low.shape
    low = low.reshape(slots // 8, 8, width)
    high = high.reshape(slots // 8, 8, width)
    first = iota(low.shape, 1) < 4
    out_ref[:, 0] = jnp.where(first, low, pltpu.roll(high, 4, 1)).astype(BF16)
    out_ref[:, 1] = jnp.where(first, pltpu.roll(low, 4, 1), high).astype(BF16)


def live(cnt_ref, slots, part):
    experts = cnt_ref.shape[0]
    spread = (iota((slots, experts), 0) // 4 == iota((slots, experts), 1)).astype(BF16)
    counts = dot(spread, cnt_ref[...].astype(F32).astype(BF16), 1, 0)
    mask = (iota((slots, counts.shape[1]), 0) % 4).astype(F32) < counts
    return mask[:, :part]


def tiles_of(ref):
    return jnp.concatenate([ref[tile] for tile in range(ref.shape[0])], axis=1)


def partial_sum(cnt_a, cnt_b, rows_a, rows_b, grads_a, grads_b):
    slots, part = rows_a.shape
    zero = jnp.zeros((), F32)
    a = jnp.where(live(cnt_a, slots, part), rows_a[...].astype(F32), zero).astype(BF16)
    b = jnp.where(live(cnt_b, slots, part), rows_b[0].astype(F32), zero).astype(BF16)
    return dot(a, tiles_of(grads_a), 0, 0) + dot(b, tiles_of(grads_b), 0, 0)


def first_kernel(me_ref, *refs):
    refs[-1][...] = partial_sum(*refs[:6]).astype(BF16)


def second_kernel(side, me_ref, *refs):
    inc, out_ref = refs[6:]
    half = inc.shape[1]
    total = partial_sum(*refs[:6])
    low, high = total[:, :half], total[:, half:]
    if side == 0:
        low = low + inc[...].astype(F32)
    else:
        high = high + inc[...].astype(F32)
    out_ref[:, :half] = low.astype(BF16)
    out_ref[:, half:] = high.astype(BF16)


def middle_kernel(me_ref, *refs):
    inc, out_ref = refs[6:]
    out_ref[...] = (partial_sum(*refs[:6]) + inc[...].astype(F32)).astype(BF16)


def last_kernel(replicas, me_ref, *refs):
    one, two, out_ref = refs[6:]
    total = partial_sum(*refs[:6]) + (one[...].astype(F32) + two[...].astype(F32))
    out_ref[:, 0, :] = total / replicas


def spread_kernel(tgt_ref, w_ref, out_ref):
    _, double, rows = out_ref.shape
    tokens = double // 2
    pairs = tgt_ref.shape[1]
    chosen = pairs // tokens
    weight = flatten_pairs(w_ref[...])
    token_of = (iota((tokens, pairs), 1) // chosen == iota((tokens, pairs), 0)).astype(BF16)
    for side in range(2):
        hit = iota((rows, pairs), 0) == tgt_ref[...] + 4 * side
        spread = jnp.where(hit, weight, jnp.zeros((), F32))
        high = spread.astype(BF16)
        low = (spread - high.astype(F32)).astype(BF16)
        out_ref[side, :tokens] = dot(token_of, high, 1, 1).astype(BF16)
        out_ref[side, tokens:] = dot(token_of, low, 1, 1).astype(BF16)


def combine_kernel(spread_ref, recv_ref, out_ref):
    tokens, model = out_ref.shape
    recv = recv_ref[...]
    for side in range(2):
        both = dot(spread_ref[side], recv, 1, 0)
        out = both[:tokens] + both[tokens:]
        out_ref[:, side * (model // 2) : (side + 1) * (model // 2)] = out.astype(BF16)


def shards(ids, weights, rows, gate_up, hidden_grad, expert_weight, interpret=False):
    def call(body, limit=16 << 20, **options):
        params = pltpu.CompilerParams(vmem_limit_bytes=limit)
        return pl.pallas_call(body, interpret=interpret, compiler_params=params, **options)

    tokens, chosen = ids.shape[1:]
    slots, model = rows.shape[2:]
    hidden = hidden_grad.shape[3]
    wide = 2 * hidden
    experts = lax.axis_size("ep")
    replicas = lax.axis_size("dp")
    ring = replicas // 2
    part = model // replicas
    pairs = tokens * chosen
    rows = rows.reshape(slots, model)
    gate_up = gate_up.reshape(slots, wide)
    hidden_grad = hidden_grad.reshape(slots, hidden)
    expert_weight = expert_weight.reshape(model, wide)
    me = lax.axis_index("dp").astype(I32).reshape(1)
    sds = jax.ShapeDtypeStruct

    counts, target = call(
        route_kernel,
        out_shape=(sds((experts, 1, 128), I32), sds((1, pairs), I32)),
        name="route",
    )(ids.reshape(tokens, chosen).T)
    counts = lax.all_to_all(counts, "ep", split_axis=0, concat_axis=0, tiled=True)

    half = model // 2
    tile = min(256, half)
    steps = half // tile
    tiles = wide // part
    trade, sent = call(
        rows_kernel,
        limit=ROWS_LIMIT,
        grid_spec=pltpu.PrefetchScalarGridSpec(
            num_scalar_prefetch=1,
            grid=(steps,),
            in_specs=[
                pl.BlockSpec((slots, wide), lambda i, me: (0, 0)),
                pl.BlockSpec((slots, hidden), lambda i, me: (0, 0)),
                pl.BlockSpec((slots, model), lambda i, me: (0, 0)),
                pl.BlockSpec((tile, wide), lambda i, me: (i, 0)),
                pl.BlockSpec((tile, wide), lambda i, me: (i + steps, 0)),
            ],
            out_specs=(
                pl.BlockSpec((tiles + ring, slots, part), lambda i, me: (0, 0, 0)),
                pl.BlockSpec((slots // 8, 2, 8, tile), lambda i, me: (0, 0, 0, i)),
            ),
            scratch_shapes=[pltpu.VMEM((slots, wide), BF16)],
        ),
        out_shape=(
            sds((tiles + ring, slots, part), BF16),
            sds((slots // 8, 2, 8, half), BF16),
        ),
        cost_estimate=cost(2 * slots * model * wide, 2 * (model * wide + 4 * slots * wide)),
        name="rows",
    )(me, gate_up, hidden_grad, rows, expert_weight, expert_weight)
    returned = lax.all_to_all(
        sent.reshape(experts, 8, half), "ep", split_axis=0, concat_axis=0, tiled=True
    )

    def neighbour(d, direction):
        turn = direction if d % 2 == 0 else -direction
        return ((d // 2 + turn) % ring) * 2 + d % 2

    partner = [(d, d ^ 1) for d in range(replicas)]
    ways = [[(d, neighbour(d, turn)) for d in range(replicas)] for turn in (1, -1)]
    other = lax.ppermute(trade, "dp", partner)
    counts = counts.reshape(experts, 128)
    other_counts = lax.ppermute(counts, "dp", partner)

    def stage(body, offset, block, incoming, out_shape, out_spec, name):
        first, count = block

        def chunk(me):
            turn = offset * (1 - 2 * lax.rem(me[0], 2))
            return lax.rem(lax.div(me[0], 2) + turn + ring, ring)

        grads = pl.BlockSpec((count, slots, part), lambda i, me: (first, 0, 0))
        specs = [
            pl.BlockSpec((experts, 128), lambda i, me: (0, 0)),
            pl.BlockSpec((experts, 128), lambda i, me: (0, 0)),
            pl.BlockSpec((slots, part), lambda i, me: (0, 2 * chunk(me) + lax.rem(me[0], 2))),
            pl.BlockSpec((1, slots, part), lambda i, me: (tiles + chunk(me), 0, 0)),
            grads,
            grads,
        ]
        specs += [pl.BlockSpec(a.shape, lambda i, me: (0, 0)) for a in incoming]
        return call(
            body,
            grid_spec=pltpu.PrefetchScalarGridSpec(
                num_scalar_prefetch=1, grid=(1,), in_specs=specs, out_specs=out_spec
            ),
            out_shape=out_shape,
            cost_estimate=cost(
                4 * part * slots * count * part, 4 * slots * count * part + 4 * part * wide
            ),
            name=name,
        )(me, counts, other_counts, rows, other, trade, other, *incoming)

    def flat(columns):
        return sds((part, columns), BF16), pl.BlockSpec((part, columns), lambda i, me: (0, 0))

    state = [None, None]
    for step in range(ring // 2):
        k = ring // 2 - step
        for side in range(2):
            if step == 0:
                block = (side, tiles // 2)
                send = stage(first_kernel, k, block, [], *flat(wide // 2), f"ring_{step}_{side}")
            else:
                body = functools.partial(second_kernel, side) if step == 1 else middle_kernel
                offset = k if side == 0 else -k
                send = stage(
                    body, offset, (0, tiles), [state[side]], *flat(wide), f"ring_{step}_{side}"
                )
            state[side] = lax.ppermute(send, "dp", ways[side])
    weight_grad = stage(
        functools.partial(last_kernel, replicas),
        0,
        (0, tiles),
        state,
        sds((part, 1, wide), F32),
        pl.BlockSpec((part, 1, wide), lambda i, me: (0, 0, 0)),
        "ring_last",
    )

    spread = call(
        spread_kernel,
        out_shape=sds((2, 2 * tokens, experts * 8), BF16),
        cost_estimate=cost(experts * 64 * pairs * tokens, 128 * experts * tokens),
        name="spread",
    )(target, weights.reshape(tokens, chosen).T)
    input_grad = call(
        combine_kernel,
        out_shape=sds((tokens, model), BF16),
        cost_estimate=cost(8 * tokens * experts * 8 * model, 2 * slots * model),
        name="combine",
    )(spread, returned.reshape(experts * 8, half))
    return input_grad.reshape(1, tokens, model), weight_grad


def solution(mesh):
    in_specs = (
        P("dp", "ep", None),
        P("dp", "ep", None),
        P("dp", "ep", None, None),
        P("dp", "ep", None, None),
        P("dp", "ep", None, None),
        P("ep", None, None),
    )
    out_specs = (P("dp", "ep", None), P("dp", "ep", None))

    return jax.shard_map(shards, mesh=mesh, in_specs=in_specs, out_specs=out_specs, check_vma=False)
```

time: 139 us -> 113 us (0.81)
  the two profiles are of different devices: /device:TPU:8 before, /device:TPU:6 now
where the time goes in v1:
time: 113 us; the launch traced here: 112 us
  starting transfers between devices  66.8 us (59%)
  waiting for transfers between devices  28.6 us (25%)
  Pallas kernels  15.5 us (14%)
    ppermute x8, starting transfers between devices, shards(): state[side] = lax.ppermute(send, 'dp', ways[side])  29.9 us
    ppermute x8, waiting for transfers between devices, shards(): state[side] = lax.ppermute(send, 'dp', ways[side])  22.7 us
    all_to_all x1, starting transfers between devices, shards(): lax.all_to_all(counts, 'ep', split_axis=0, concat_axis=0, tiled=True)  22.5 us
    all_to_all x1, starting transfers between devices, shards(): lax.all_to_all(sent.reshape(experts, 8, half), 'ep', split_axis=0, concat...  10.2 us
    pallas_call x1, Pallas kernels, shards(): call(rows_kernel, limit=ROWS_LIMIT, grid_spec=pltpu.PrefetchScalarGridSpe...  7.38 us
    pallas_call x9, Pallas kernels, stage(): call(body, grid_spec=pltpu.PrefetchScalarGridSpec(num_scalar_prefetch=1,...  5.8 us
    all_to_all x1, waiting for transfers between devices, shards(): lax.all_to_all(counts, 'ep', split_axis=0, concat_axis=0, tiled=True)  5.1 us
    ppermute x1, starting transfers between devices, shards(): other_counts = lax.ppermute(counts, 'dp', partner)  2.41 us
  transfers between devices with their start and end apart: 12, of which 7 were waited for; matrix products, arithmetic and copies ran while one was open for 0% of the time, Pallas kernels for 12%

profile of v1, /device:TPU:6, one launch (start us, length us, event | category | flops | bytes accessed | tf_op | source)
XLA Modules:
  0.0 112.5 jit_solution(13598666980924206557)
XLA Ops:
  0.6 0.0 copy-start.3
  0.6 0.7 copy-done.3
  1.3 0.8 route.1
  2.1 22.5 %all-to-all-start.1 = ((s32[64,1,128]{2,1,0:T(1,128)}), s32[64,1,128]{2,1,0:T(1,128)S(1)}, u32[]{:S(2)}, u32[]{:S(2)}) async-start(s32[64,1,128]{2,1,0:T(1,128)} %get-tuple-element.8), calls=%async_computation.1 | async-start | bytes 65536 | tf_op jit(solution)/shard_map/all_to_all | solution.py:182
  24.6 0.0 copy-start.1
  24.6 7.4 %rows.1 = (bf16[20,256,128]{2,1,0:T(8,128)(2,1)}, bf16[32,2,8,1024]{3,2,1,0:T(8,128)(2,1)}) custom-call(s32[1]{0:T(128)} %bitcast.4.me_ref, bf16[256,1536]{1,0:T(8,128)(2,1)} %bitcast.41, bf16[256,768]{1,0:T(8,128)(2,1)} %bitcast.42, bf16[256,2048]{1,0:T(8,128)(2,1)} %bitcast.15, bf16[2048,1536]{1,0:T(8,128)(2,1)} %bitcast.38, bf16[2048,1536]{1,0:T(8,128)(2,1)} %bitcast.39), custom_call_target="tpu_custom_call" | custom-call | flops 1610612736 | bytes 9437184 | tf_op jit(solution)/shard_map/rows/pallas_call | solution.py:188
  32.0 0.0 copy-start
  32.0 5.1 %all-to-all-done.1 = s32[64,1,128]{2,1,0:T(1,128)S(1)} async-done(((s32[64,1,128]{2,1,0:T(1,128)}), s32[64,1,128]{2,1,0:T(1,128)S(1)}, u32[]{:S(2)}, u32[]{:S(2)}) %all-to-all-start.1) | async-done | bytes 32800 | tf_op jit(solution)/shard_map/all_to_all | solution.py:182
  37.1 10.2 %all-to-all-start = ((bf16[64,8,1024]{2,1,0:T(8,128)(2,1)}), bf16[64,8,1024]{2,1,0:T(8,128)(2,1)S(1)}, u32[]{:S(2)}, u32[]{:S(2)}) async-start(bf16[64,8,1024]{2,1,0:T(8,128)(2,1)} %bitcast.40), calls=%async_computation | async-start | bytes 2097152 | tf_op jit(solution)/shard_map/all_to_all | solution.py:214
  47.3 0.0 copy-done
  47.3 1.9 %collective-permute-start.1 = (bf16[20,256,128]{2,1,0:T(8,128)(2,1)S(1)}, bf16[20,256,128]{2,1,0:T(8,128)(2,1)S(1)}, u32[]{:S(2)}, u32[]{:S(2)}) collective-permute-start(bf16[20,256,128]{2,1,0:T(8,128)(2,1)S(1)} %copy-done), channel_id=1, source_target_pairs={{0,64},{64,0},{128,192},{192,128},{256,320},{320,256},{384,448},{4... | collective-permute-start | bytes 3932168 | tf_op jit(solution)/shard_map/ppermute | solution.py:224
  49.2 2.4 %collective-permute-start = (s32[64,128]{1,0:T(8,128)S(1)}, s32[64,128]{1,0:T(8,128)S(1)}, u32[]{:S(2)}, u32[]{:S(2)}) collective-permute-start(s32[64,128]{1,0:T(8,128)S(1)} %bitcast.26), channel_id=1, source_target_pairs={{0,64},{64,0},{128,192},{192,128},{256,320},{320,256},{384,448},{4... | collective-permute-start | bytes 98312 | tf_op jit(solution)/shard_map/ppermute | solution.py:226
  51.6 0.8 collective-permute-done.refs_1_
  52.5 0.0 collective-permute-done.1.refs_3_.refs_5_
  52.5 0.0 copy-done.1
  52.5 0.4 ring_0_1.1
  52.9 5.4 %collective-permute-start.6 = (bf16[128,768]{1,0:T(8,128)(2,1)S(1)}, bf16[128,768]{1,0:T(8,128)(2,1)S(1)}, u32[]{:S(2)}, u32[]{:S(2)}) collective-permute-start(bf16[128,768]{1,0:T(8,128)(2,1)S(1)} %ring_0_1.1), channel_id=1, source_target_pairs={{0,896},{64,192},{128,0},{192,320},{256,128},{320,448},{384,256},{... | collective-permute-start | bytes 589832 | tf_op jit(solution)/shard_map/ppermute | solution.py:273
  58.3 0.4 ring_0_0.1
  58.8 1.9 %collective-permute-start.2 = (bf16[128,768]{1,0:T(8,128)(2,1)S(1)}, bf16[128,768]{1,0:T(8,128)(2,1)S(1)}, u32[]{:S(2)}, u32[]{:S(2)}) collective-permute-start(bf16[128,768]{1,0:T(8,128)(2,1)S(1)} %ring_0_0.1), channel_id=1, source_target_pairs={{0,128},{64,960},{128,256},{192,64},{256,384},{320,192},{384,512},... | collective-permute-start | bytes 589832 | tf_op jit(solution)/shard_map/ppermute | solution.py:273
  60.7 1.1 %collective-permute-done.6.refs_6_ = bf16[128,768]{1,0:T(8,128)(2,1)S(1)} collective-permute-done((bf16[128,768]{1,0:T(8,128)(2,1)S(1)}, bf16[128,768]{1,0:T(8,128)(2,1)S(1)}, u32[]{:S(2)}, u32[]{:S(2)}) %collective-permute-start.6) | collective-permute-done | bytes 196640 | tf_op jit(solution)/shard_map/ppermute | solution.py:273
  61.8 0.6 ring_1_1.1
  62.4 5.6 %collective-permute-start.7 = (bf16[128,1536]{1,0:T(8,128)(2,1)S(1)}, bf16[128,1536]{1,0:T(8,128)(2,1)S(1)}, u32[]{:S(2)}, u32[]{:S(2)}) collective-permute-start(bf16[128,1536]{1,0:T(8,128)(2,1)S(1)} %ring_1_1.1), channel_id=1, source_target_pairs={{0,896},{64,192},{128,0},{192,320},{256,128},{320,448},{384,256},{... | collective-permute-start | bytes 1179656 | tf_op jit(solution)/shard_map/ppermute | solution.py:273
  68.0 0.0 collective-permute-done.2.refs_6_
  68.0 0.6 ring_1_0.1
  68.6 1.9 %collective-permute-start.3 = (bf16[128,1536]{1,0:T(8,128)(2,1)S(1)}, bf16[128,1536]{1,0:T(8,128)(2,1)S(1)}, u32[]{:S(2)}, u32[]{:S(2)}) collective-permute-start(bf16[128,1536]{1,0:T(8,128)(2,1)S(1)} %ring_1_0.1), channel_id=1, source_target_pairs={{0,128},{64,960},{128,256},{192,64},{256,384},{320,192},{384,512},... | collective-permute-start | bytes 1179656 | tf_op jit(solution)/shard_map/ppermute | solution.py:273
  70.5 6.1 %collective-permute-done.7.refs_6_ = bf16[128,1536]{1,0:T(8,128)(2,1)S(1)} collective-permute-done((bf16[128,1536]{1,0:T(8,128)(2,1)S(1)}, bf16[128,1536]{1,0:T(8,128)(2,1)S(1)}, u32[]{:S(2)}, u32[]{:S(2)}) %collective-permute-start.7) | collective-permute-done | bytes 393248 | tf_op jit(solution)/shard_map/ppermute | solution.py:273
  76.6 0.6 ring_2_1.1
  77.1 5.6 %collective-permute-start.8 = (bf16[128,1536]{1,0:T(8,128)(2,1)S(1)}, bf16[128,1536]{1,0:T(8,128)(2,1)S(1)}, u32[]{:S(2)}, u32[]{:S(2)}) collective-permute-start(bf16[128,1536]{1,0:T(8,128)(2,1)S(1)} %ring_2_1.1), channel_id=1, source_target_pairs={{0,896},{64,192},{128,0},{192,320},{256,128},{320,448},{384,256},{... | collective-permute-start | bytes 1179656 | tf_op jit(solution)/shard_map/ppermute | solution.py:273
  82.7 0.0 collective-permute-done.3.refs_6_
  82.8 0.6 ring_2_0.1
  83.3 1.9 %collective-permute-start.4 = (bf16[128,1536]{1,0:T(8,128)(2,1)S(1)}, bf16[128,1536]{1,0:T(8,128)(2,1)S(1)}, u32[]{:S(2)}, u32[]{:S(2)}) collective-permute-start(bf16[128,1536]{1,0:T(8,128)(2,1)S(1)} %ring_2_0.1), channel_id=1, source_target_pairs={{0,128},{64,960},{128,256},{192,64},{256,384},{320,192},{384,512},... | collective-permute-start | bytes 1179656 | tf_op jit(solution)/shard_map/ppermute | solution.py:273
  85.2 6.9 %collective-permute-done.8.refs_6_ = bf16[128,1536]{1,0:T(8,128)(2,1)S(1)} collective-permute-done((bf16[128,1536]{1,0:T(8,128)(2,1)S(1)}, bf16[128,1536]{1,0:T(8,128)(2,1)S(1)}, u32[]{:S(2)}, u32[]{:S(2)}) %collective-permute-start.8) | collective-permute-done | bytes 393248 | tf_op jit(solution)/shard_map/ppermute | solution.py:273
  92.2 0.6 ring_3_1.1
  92.7 0.0 copy-start.2
  92.7 5.6 %collective-permute-start.9 = (bf16[128,1536]{1,0:T(8,128)(2,1)S(1)}, bf16[128,1536]{1,0:T(8,128)(2,1)S(1)}, u32[]{:S(2)}, u32[]{:S(2)}) collective-permute-start(bf16[128,1536]{1,0:T(8,128)(2,1)S(1)} %ring_3_1.1), channel_id=1, source_target_pairs={{0,896},{64,192},{128,0},{192,320},{256,128},{320,448},{384,256},{... | collective-permute-start | bytes 1179656 | tf_op jit(solution)/shard_map/ppermute | solution.py:273
  98.3 0.0 collective-permute-done.4.refs_6_
  98.4 0.6 ring_3_0.1
  98.9 1.9 %collective-permute-start.5 = (bf16[128,1536]{1,0:T(8,128)(2,1)S(1)}, bf16[128,1536]{1,0:T(8,128)(2,1)S(1)}, u32[]{:S(2)}, u32[]{:S(2)}) collective-permute-start(bf16[128,1536]{1,0:T(8,128)(2,1)S(1)} %ring_3_0.1), channel_id=1, source_target_pairs={{0,128},{64,960},{128,256},{192,64},{256,384},{320,192},{384,512},... | collective-permute-start | bytes 1179656 | tf_op jit(solution)/shard_map/ppermute | solution.py:273
  100.9 0.0 copy-done.2
  100.9 0.4 spread.1.spread_ref
  101.2 5.8 %collective-permute-done.9.refs_7_ = bf16[128,1536]{1,0:T(8,128)(2,1)S(1)} collective-permute-done((bf16[128,1536]{1,0:T(8,128)(2,1)S(1)}, bf16[128,1536]{1,0:T(8,128)(2,1)S(1)}, u32[]{:S(2)}, u32[]{:S(2)}) %collective-permute-start.9) | collective-permute-done | bytes 393248 | tf_op jit(solution)/shard_map/ppermute | solution.py:273
  107.0 2.8 %collective-permute-done.5.refs_6_ = bf16[128,1536]{1,0:T(8,128)(2,1)S(1)} collective-permute-done((bf16[128,1536]{1,0:T(8,128)(2,1)S(1)}, bf16[128,1536]{1,0:T(8,128)(2,1)S(1)}, u32[]{:S(2)}, u32[]{:S(2)}) %collective-permute-start.5) | collective-permute-done | bytes 393248 | tf_op jit(solution)/shard_map/ppermute | solution.py:273
  109.8 1.6 %ring_last.1 = f32[128,1,1536]{2,1,0:T(1,128)} custom-call(s32[1]{0:T(128)} %bitcast.4.me_ref, s32[64,128]{1,0:T(8,128)S(1)} %bitcast.35, s32[64,128]{1,0:T(8,128)S(1)} %collective-permute-done.refs_1_, bf16[256,2048]{1,0:T(8,128)(2,1)S(1)} %bitcast.24, bf16[20,256,128]{2,1,0:T(8,128)(2,1)S(1)} %collective-permute-done.1.refs_3_.refs_5_, ...), custom_call_target="tpu_custom_call" | custom-call | flops 201326592 | bytes 2359296 | tf_op jit(solution)/shard_map/ring_last/pallas_call | solution.py:245
  111.4 0.0 all-to-all-done
  111.4 1.1 combine.1
Async XLA Ops:
  0.6 0.7 copy-start.3
  2.1 35.0 %all-to-all-start.1 = ((s32[64,1,128]{2,1,0:T(1,128)}), s32[64,1,128]{2,1,0:T(1,128)S(1)}, u32[]{:S(2)}, u32[]{:S(2)}) async-start(s32[64,1,128]{2,1,0:T(1,128)} %get-tuple-element.8), calls=%async_computation.1 | async-start | bytes 65536 | tf_op jit(solution)/shard_map/all_to_all | solution.py:182
  24.6 27.9 %copy-start.1 = (bf16[1,1,256,2048]{3,2,1,0:T(8,128)(2,1)S(1)}, bf16[1,1,256,2048]{3,2,1,0:T(8,128)(2,1)}, u32[]{:S(2)}) copy-start(bf16[1,1,256,2048]{3,2,1,0:T(8,128)(2,1)} %param.8) | copy-start | bytes 3145732
  32.0 15.3 %copy-start = (bf16[20,256,128]{2,1,0:T(8,128)(2,1)S(1)}, bf16[20,256,128]{2,1,0:T(8,128)(2,1)}, u32[]{:S(2)}) copy-start(bf16[20,256,128]{2,1,0:T(8,128)(2,1)} %get-tuple-element.9.refs_4_) | copy-start | bytes 3932164
  37.1 74.3 %all-to-all-start = ((bf16[64,8,1024]{2,1,0:T(8,128)(2,1)}), bf16[64,8,1024]{2,1,0:T(8,128)(2,1)S(1)}, u32[]{:S(2)}, u32[]{:S(2)}) async-start(bf16[64,8,1024]{2,1,0:T(8,128)(2,1)} %bitcast.40), calls=%async_computation | async-start | bytes 2097152 | tf_op jit(solution)/shard_map/all_to_all | solution.py:214
  47.3 5.2 %collective-permute-start.1 = (bf16[20,256,128]{2,1,0:T(8,128)(2,1)S(1)}, bf16[20,256,128]{2,1,0:T(8,128)(2,1)S(1)}, u32[]{:S(2)}, u32[]{:S(2)}) collective-permute-start(bf16[20,256,128]{2,1,0:T(8,128)(2,1)S(1)} %copy-done), channel_id=1, source_target_pairs={{0,64},{64,0},{128,192},{192,128},{256,320},{320,256},{384,448},{4... | collective-permute-start | bytes 3932168 | tf_op jit(solution)/shard_map/ppermute | solution.py:224
  49.2 3.3 %collective-permute-start = (s32[64,128]{1,0:T(8,128)S(1)}, s32[64,128]{1,0:T(8,128)S(1)}, u32[]{:S(2)}, u32[]{:S(2)}) collective-permute-start(s32[64,128]{1,0:T(8,128)S(1)} %bitcast.26), channel_id=1, source_target_pairs={{0,64},{64,0},{128,192},{192,128},{256,320},{320,256},{384,448},{4... | collective-permute-start | bytes 98312 | tf_op jit(solution)/shard_map/ppermute | solution.py:226
  52.9 8.9 %collective-permute-start.6 = (bf16[128,768]{1,0:T(8,128)(2,1)S(1)}, bf16[128,768]{1,0:T(8,128)(2,1)S(1)}, u32[]{:S(2)}, u32[]{:S(2)}) collective-permute-start(bf16[128,768]{1,0:T(8,128)(2,1)S(1)} %ring_0_1.1), channel_id=1, source_target_pairs={{0,896},{64,192},{128,0},{192,320},{256,128},{320,448},{384,256},{... | collective-permute-start | bytes 589832 | tf_op jit(solution)/shard_map/ppermute | solution.py:273
  58.8 9.2 %collective-permute-start.2 = (bf16[128,768]{1,0:T(8,128)(2,1)S(1)}, bf16[128,768]{1,0:T(8,128)(2,1)S(1)}, u32[]{:S(2)}, u32[]{:S(2)}) collective-permute-start(bf16[128,768]{1,0:T(8,128)(2,1)S(1)} %ring_0_0.1), channel_id=1, source_target_pairs={{0,128},{64,960},{128,256},{192,64},{256,384},{320,192},{384,512},... | collective-permute-start | bytes 589832 | tf_op jit(solution)/shard_map/ppermute | solution.py:273
  62.4 14.2 %collective-permute-start.7 = (bf16[128,1536]{1,0:T(8,128)(2,1)S(1)}, bf16[128,1536]{1,0:T(8,128)(2,1)S(1)}, u32[]{:S(2)}, u32[]{:S(2)}) collective-permute-start(bf16[128,1536]{1,0:T(8,128)(2,1)S(1)} %ring_1_1.1), channel_id=1, source_target_pairs={{0,896},{64,192},{128,0},{192,320},{256,128},{320,448},{384,256},{... | collective-permute-start | bytes 1179656 | tf_op jit(solution)/shard_map/ppermute | solution.py:273
  68.6 14.2 %collective-permute-start.3 = (bf16[128,1536]{1,0:T(8,128)(2,1)S(1)}, bf16[128,1536]{1,0:T(8,128)(2,1)S(1)}, u32[]{:S(2)}, u32[]{:S(2)}) collective-permute-start(bf16[128,1536]{1,0:T(8,128)(2,1)S(1)} %ring_1_0.1), channel_id=1, source_target_pairs={{0,128},{64,960},{128,256},{192,64},{256,384},{320,192},{384,512},... | collective-permute-start | bytes 1179656 | tf_op jit(solution)/shard_map/ppermute | solution.py:273
  77.1 15.0 %collective-permute-start.8 = (bf16[128,1536]{1,0:T(8,128)(2,1)S(1)}, bf16[128,1536]{1,0:T(8,128)(2,1)S(1)}, u32[]{:S(2)}, u32[]{:S(2)}) collective-permute-start(bf16[128,1536]{1,0:T(8,128)(2,1)S(1)} %ring_2_1.1), channel_id=1, source_target_pairs={{0,896},{64,192},{128,0},{192,320},{256,128},{320,448},{384,256},{... | collective-permute-start | bytes 1179656 | tf_op jit(solution)/shard_map/ppermute | solution.py:273
  83.3 15.0 %collective-permute-start.4 = (bf16[128,1536]{1,0:T(8,128)(2,1)S(1)}, bf16[128,1536]{1,0:T(8,128)(2,1)S(1)}, u32[]{:S(2)}, u32[]{:S(2)}) collective-permute-start(bf16[128,1536]{1,0:T(8,128)(2,1)S(1)} %ring_2_0.1), channel_id=1, source_target_pairs={{0,128},{64,960},{128,256},{192,64},{256,384},{320,192},{384,512},... | collective-permute-start | bytes 1179656 | tf_op jit(solution)/shard_map/ppermute | solution.py:273
  92.7 8.1 %copy-start.2 = (f32[1,16,8]{1,2,0:T(8,128)S(1)}, f32[1,16,8]{1,2,0:T(8,128)}, u32[]{:S(2)}) copy-start(f32[1,16,8]{1,2,0:T(8,128)} %param.7) | copy-start | bytes 1540
  92.7 14.3 %collective-permute-start.9 = (bf16[128,1536]{1,0:T(8,128)(2,1)S(1)}, bf16[128,1536]{1,0:T(8,128)(2,1)S(1)}, u32[]{:S(2)}, u32[]{:S(2)}) collective-permute-start(bf16[128,1536]{1,0:T(8,128)(2,1)S(1)} %ring_3_1.1), channel_id=1, source_target_pairs={{0,896},{64,192},{128,0},{192,320},{256,128},{320,448},{384,256},{... | collective-permute-start | bytes 1179656 | tf_op jit(solution)/shard_map/ppermute | solution.py:273
  98.9 10.9 %collective-permute-start.5 = (bf16[128,1536]{1,0:T(8,128)(2,1)S(1)}, bf16[128,1536]{1,0:T(8,128)(2,1)S(1)}, u32[]{:S(2)}, u32[]{:S(2)}) collective-permute-start(bf16[128,1536]{1,0:T(8,128)(2,1)S(1)} %ring_3_0.1), channel_id=1, source_target_pairs={{0,128},{64,960},{128,256},{192,64},{256,384},{320,192},{384,512},... | collective-permute-start | bytes 1179656 | tf_op jit(solution)/shard_map/ppermute | solution.py:273

commit v2 on v1

--- a/solution.py
+++ b/solution.py
@@ -46,7 +46,7 @@
     cnt_ref[:, 0, :] = jnp.broadcast_to(counts, (experts, cnt_ref.shape[2]))
 
 
-def rows_kernel(me_ref, gu_ref, hg_ref, rows_ref, wlo_ref, whi_ref, trade_ref, out_ref, grads_ref):
+def rows_kernel(me_ref, gu_ref, hg_ref, rows_ref, wlo_ref, whi_ref, trade_ref, mine_ref, out_ref, grads_ref):
     @pl.when(pl.program_id(0) == 0)
     def _():
         hidden = hg_ref.shape[1]
@@ -63,11 +63,10 @@
         second = lax.rem(me_ref[0], 2) == 0
         for chunk in range(trade_ref.shape[0] - tiles):
             start = 2 * chunk * part
-            trade_ref[tiles + chunk] = jnp.where(
-                second,
-                rows_ref[:, start + part : start + 2 * part],
-                rows_ref[:, start : start + part],
-            )
+            even = rows_ref[:, start : start + part]
+            odd = rows_ref[:, start + part : start + 2 * part]
+            trade_ref[tiles + chunk] = jnp.where(second, odd, even)
+            mine_ref[chunk] = jnp.where(second, even, odd)
 
     grads = grads_ref[...]
     low = dot(grads, wlo_ref[...], 1, 1)
@@ -93,9 +92,9 @@
 
 
 def partial_sum(cnt_a, cnt_b, rows_a, rows_b, grads_a, grads_b):
-    slots, part = rows_a.shape
+    slots, part = rows_a.shape[1:]
     zero = jnp.zeros((), F32)
-    a = jnp.where(live(cnt_a, slots, part), rows_a[...].astype(F32), zero).astype(BF16)
+    a = jnp.where(live(cnt_a, slots, part), rows_a[0].astype(F32), zero).astype(BF16)
     b = jnp.where(live(cnt_b, slots, part), rows_b[0].astype(F32), zero).astype(BF16)
     return dot(a, tiles_of(grads_a), 0, 0) + dot(b, tiles_of(grads_b), 0, 0)
 
@@ -122,9 +121,12 @@
     out_ref[...] = (partial_sum(*refs[:6]) + inc[...].astype(F32)).astype(BF16)
 
 
-def last_kernel(replicas, me_ref, *refs):
-    one, two, out_ref = refs[6:]
-    total = partial_sum(*refs[:6]) + (one[...].astype(F32) + two[...].astype(F32))
+def own_kernel(me_ref, *refs):
+    refs[-1][...] = partial_sum(*refs[:6])
+
+
+def last_kernel(replicas, own_ref, one_ref, two_ref, out_ref):
+    total = own_ref[...] + (one_ref[...].astype(F32) + two_ref[...].astype(F32))
     out_ref[:, 0, :] = total / replicas
 
 
@@ -176,6 +178,7 @@
 
     counts, target = call(
         route_kernel,
+        limit=60 << 20,
         out_shape=(sds((experts, 1, 128), I32), sds((1, pairs), I32)),
         name="route",
     )(ids.reshape(tokens, chosen).T)
@@ -185,7 +188,7 @@
     tile = min(256, half)
     steps = half // tile
     tiles = wide // part
-    trade, sent = call(
+    trade, mine, sent = call(
         rows_kernel,
         limit=ROWS_LIMIT,
         grid_spec=pltpu.PrefetchScalarGridSpec(
@@ -200,12 +203,14 @@
             ],
             out_specs=(
                 pl.BlockSpec((tiles + ring, slots, part), lambda i, me: (0, 0, 0)),
+                pl.BlockSpec((ring, slots, part), lambda i, me: (0, 0, 0)),
                 pl.BlockSpec((slots // 8, 2, 8, tile), lambda i, me: (0, 0, 0, i)),
             ),
             scratch_shapes=[pltpu.VMEM((slots, wide), BF16)],
         ),
         out_shape=(
             sds((tiles + ring, slots, part), BF16),
+            sds((ring, slots, part), BF16),
             sds((slots // 8, 2, 8, half), BF16),
         ),
         cost_estimate=cost(2 * slots * model * wide, 2 * (model * wide + 4 * slots * wide)),
@@ -236,7 +241,7 @@
         specs = [
             pl.BlockSpec((experts, 128), lambda i, me: (0, 0)),
             pl.BlockSpec((experts, 128), lambda i, me: (0, 0)),
-            pl.BlockSpec((slots, part), lambda i, me: (0, 2 * chunk(me) + lax.rem(me[0], 2))),
+            pl.BlockSpec((1, slots, part), lambda i, me: (chunk(me), 0, 0)),
             pl.BlockSpec((1, slots, part), lambda i, me: (tiles + chunk(me), 0, 0)),
             grads,
             grads,
@@ -252,11 +257,20 @@
                 4 * part * slots * count * part, 4 * slots * count * part + 4 * part * wide
             ),
             name=name,
-        )(me, counts, other_counts, rows, other, trade, other, *incoming)
+        )(me, counts, other_counts, mine, other, trade, other, *incoming)
 
     def flat(columns):
         return sds((part, columns), BF16), pl.BlockSpec((part, columns), lambda i, me: (0, 0))
 
+    own = stage(
+        own_kernel,
+        0,
+        (0, tiles),
+        [],
+        sds((part, wide), F32),
+        pl.BlockSpec((part, wide), lambda i, me: (0, 0)),
+        "own",
+    )
     state = [None, None]
     for step in range(ring // 2):
         k = ring // 2 - step
@@ -271,15 +285,12 @@
                     body, offset, (0, tiles), [state[side]], *flat(wide), f"ring_{step}_{side}"
                 )
             state[side] = lax.ppermute(send, "dp", ways[side])
-    weight_grad = stage(
+    weight_grad = call(
         functools.partial(last_kernel, replicas),
-        0,
-        (0, tiles),
-        state,
-        sds((part, 1, wide), F32),
-        pl.BlockSpec((part, 1, wide), lambda i, me: (0, 0, 0)),
-        "ring_last",
-    )
+        out_shape=sds((part, 1, wide), F32),
+        cost_estimate=cost(3 * part * wide, 12 * part * wide),
+        name="ring_last",
+    )(own, *state)
 
     spread = call(
         spread_kernel,

time: 113 us -> 113 us (level)
  Pallas kernels: 15.5 us -> 16.7 us
    pallas_call x1 -> x2, Pallas kernels: 0.81 us -> 2.65 us  [the longest x1 1.51 us: shards(): call(route_kernel, limit=60 << 20, out_shape=(sds((experts, 1, 128), I32)...]
  transfers between devices with their start and end apart: 12 -> 12, of which waited for: 7 -> 7; matrix products, arithmetic and copies ran while one was open for 0% -> 0% of each run, Pallas kernels for 12% -> 13%
where the time goes in v2:
time: 113 us; the launch traced here: 112 us
  starting transfers between devices  67.2 us (59%)
  waiting for transfers between devices  27.7 us (25%)
  Pallas kernels  16.7 us (15%)
    ppermute x8, starting transfers between devices, shards(): state[side] = lax.ppermute(send, 'dp', ways[side])  29.9 us
    all_to_all x1, starting transfers between devices, shards(): lax.all_to_all(counts, 'ep', split_axis=0, concat_axis=0, tiled=True)  22.5 us
    ppermute x8, waiting for transfers between devices, shards(): state[side] = lax.ppermute(send, 'dp', ways[side])  22.1 us
    all_to_all x1, starting transfers between devices, shards(): lax.all_to_all(sent.reshape(experts, 8, half), 'ep', split_axis=0, concat...  10.6 us
    pallas_call x1, Pallas kernels, shards(): call(rows_kernel, limit=ROWS_LIMIT, grid_spec=pltpu.PrefetchScalarGridSpe...  7.76 us
    pallas_call x9, Pallas kernels, stage(): call(body, grid_spec=pltpu.PrefetchScalarGridSpec(num_scalar_prefetch=1,...  4.77 us
    all_to_all x1, waiting for transfers between devices, shards(): lax.all_to_all(counts, 'ep', split_axis=0, concat_axis=0, tiled=True)  4.73 us
    ppermute x1, starting transfers between devices, shards(): other_counts = lax.ppermute(counts, 'dp', partner)  2.41 us
  transfers between devices with their start and end apart: 12, of which 7 were waited for; matrix products, arithmetic and copies ran while one was open for 0% of the time, Pallas kernels for 13%

profile of v2, /device:TPU:6, one launch (start us, length us, event | category | flops | bytes accessed | tf_op | source)
XLA Modules:
  0.0 112.4 jit_solution(10212059007190753316)
XLA Ops:
  0.6 1.5 %route.1 = (s32[64,1,128]{2,1,0:T(1,128)}, s32[1,128]{1,0:T(1,128)}) custom-call(s32[8,16]{1,0:T(8,128)} %bitcast.34), custom_call_target="tpu_custom_call" | custom-call | tf_op jit(solution)/shard_map/route/pallas_call | solution.py:179
  2.1 22.5 %all-to-all-start.1 = ((s32[64,1,128]{2,1,0:T(1,128)}), s32[64,1,128]{2,1,0:T(1,128)S(1)}, u32[]{:S(2)}, u32[]{:S(2)}) async-start(s32[64,1,128]{2,1,0:T(1,128)} %get-tuple-element.9), calls=%async_computation.1 | async-start | bytes 65536 | tf_op jit(solution)/shard_map/all_to_all | solution.py:185
  24.6 7.8 %rows.1 = (bf16[20,256,128]{2,1,0:T(8,128)(2,1)}, bf16[8,256,128]{2,1,0:T(8,128)(2,1)}, bf16[32,2,8,1024]{3,2,1,0:T(8,128)(2,1)}) custom-call(s32[1]{0:T(128)} %bitcast.4.me_ref, bf16[256,1536]{1,0:T(8,128)(2,1)} %bitcast.31, bf16[256,768]{1,0:T(8,128)(2,1)} %bitcast.32, bf16[256,2048]{1,0:T(8,128)(2,1)} %bitcast.29, bf16[2048,1536]{1,0:T(8,128)(2,1)} %bitcast.27, ...), custom_call_target="tpu_custom_call" | custom-call | flops 1610612736 | bytes 9437184 | tf_op jit(solution)/shard_map/rows/pallas_call | solution.py:191
  32.4 0.0 copy-start
  32.4 0.0 copy-start.1
  32.4 4.7 %all-to-all-done.1 = s32[64,1,128]{2,1,0:T(1,128)S(1)} async-done(((s32[64,1,128]{2,1,0:T(1,128)}), s32[64,1,128]{2,1,0:T(1,128)S(1)}, u32[]{:S(2)}, u32[]{:S(2)}) %all-to-all-start.1) | async-done | bytes 32800 | tf_op jit(solution)/shard_map/all_to_all | solution.py:185
  37.1 10.6 %all-to-all-start = ((bf16[64,8,1024]{2,1,0:T(8,128)(2,1)}), bf16[64,8,1024]{2,1,0:T(8,128)(2,1)S(1)}, u32[]{:S(2)}, u32[]{:S(2)}) async-start(bf16[64,8,1024]{2,1,0:T(8,128)(2,1)} %bitcast.30), calls=%async_computation | async-start | bytes 2097152 | tf_op jit(solution)/shard_map/all_to_all | solution.py:219
  47.7 0.0 copy-done
  47.7 1.9 %collective-permute-start.1 = (bf16[20,256,128]{2,1,0:T(8,128)(2,1)S(1)}, bf16[20,256,128]{2,1,0:T(8,128)(2,1)S(1)}, u32[]{:S(2)}, u32[]{:S(2)}) collective-permute-start(bf16[20,256,128]{2,1,0:T(8,128)(2,1)S(1)} %copy-done), channel_id=1, source_target_pairs={{0,64},{64,0},{128,192},{192,128},{256,320},{320,256},{384,448},{4... | collective-permute-start | bytes 3932168 | tf_op jit(solution)/shard_map/ppermute | solution.py:229
  49.6 2.4 %collective-permute-start = (s32[64,128]{1,0:T(8,128)S(1)}, s32[64,128]{1,0:T(8,128)S(1)}, u32[]{:S(2)}, u32[]{:S(2)}) collective-permute-start(s32[64,128]{1,0:T(8,128)S(1)} %bitcast.16), channel_id=1, source_target_pairs={{0,64},{64,0},{128,192},{192,128},{256,320},{320,256},{384,448},{4... | collective-permute-start | bytes 98312 | tf_op jit(solution)/shard_map/ppermute | solution.py:231
  52.0 0.8 collective-permute-done.refs_1_
  52.9 0.0 collective-permute-done.1.refs_3_.refs_5_
  52.9 0.0 copy-done.1
  52.9 0.4 ring_0_1.1
  53.3 5.4 %collective-permute-start.6 = (bf16[128,768]{1,0:T(8,128)(2,1)S(1)}, bf16[128,768]{1,0:T(8,128)(2,1)S(1)}, u32[]{:S(2)}, u32[]{:S(2)}) collective-permute-start(bf16[128,768]{1,0:T(8,128)(2,1)S(1)} %ring_0_1.1), channel_id=1, source_target_pairs={{0,896},{64,192},{128,0},{192,320},{256,128},{320,448},{384,256},{... | collective-permute-start | bytes 589832 | tf_op jit(solution)/shard_map/ppermute | solution.py:287
  58.7 0.4 ring_0_0.1
  59.2 1.9 %collective-permute-start.2 = (bf16[128,768]{1,0:T(8,128)(2,1)S(1)}, bf16[128,768]{1,0:T(8,128)(2,1)S(1)}, u32[]{:S(2)}, u32[]{:S(2)}) collective-permute-start(bf16[128,768]{1,0:T(8,128)(2,1)S(1)} %ring_0_0.1), channel_id=1, source_target_pairs={{0,128},{64,960},{128,256},{192,64},{256,384},{320,192},{384,512},... | collective-permute-start | bytes 589832 | tf_op jit(solution)/shard_map/ppermute | solution.py:287
  61.1 1.1 %collective-permute-done.6.refs_6_ = bf16[128,768]{1,0:T(8,128)(2,1)S(1)} collective-permute-done((bf16[128,768]{1,0:T(8,128)(2,1)S(1)}, bf16[128,768]{1,0:T(8,128)(2,1)S(1)}, u32[]{:S(2)}, u32[]{:S(2)}) %collective-permute-start.6) | collective-permute-done | bytes 196640 | tf_op jit(solution)/shard_map/ppermute | solution.py:287
  62.2 0.6 ring_1_1.1
  62.8 5.6 %collective-permute-start.7 = (bf16[128,1536]{1,0:T(8,128)(2,1)S(1)}, bf16[128,1536]{1,0:T(8,128)(2,1)S(1)}, u32[]{:S(2)}, u32[]{:S(2)}) collective-permute-start(bf16[128,1536]{1,0:T(8,128)(2,1)S(1)} %ring_1_1.1), channel_id=1, source_target_pairs={{0,896},{64,192},{128,0},{192,320},{256,128},{320,448},{384,256},{... | collective-permute-start | bytes 1179656 | tf_op jit(solution)/shard_map/ppermute | solution.py:287
  68.4 0.0 collective-permute-done.2.refs_6_
  68.4 0.6 ring_1_0.1
  69.0 1.9 %collective-permute-start.3 = (bf16[128,1536]{1,0:T(8,128)(2,1)S(1)}, bf16[128,1536]{1,0:T(8,128)(2,1)S(1)}, u32[]{:S(2)}, u32[]{:S(2)}) collective-permute-start(bf16[128,1536]{1,0:T(8,128)(2,1)S(1)} %ring_1_0.1), channel_id=1, source_target_pairs={{0,128},{64,960},{128,256},{192,64},{256,384},{320,192},{384,512},... | collective-permute-start | bytes 1179656 | tf_op jit(solution)/shard_map/ppermute | solution.py:287
  70.9 6.1 %collective-permute-done.7.refs_6_ = bf16[128,1536]{1,0:T(8,128)(2,1)S(1)} collective-permute-done((bf16[128,1536]{1,0:T(8,128)(2,1)S(1)}, bf16[128,1536]{1,0:T(8,128)(2,1)S(1)}, u32[]{:S(2)}, u32[]{:S(2)}) %collective-permute-start.7) | collective-permute-done | bytes 393248 | tf_op jit(solution)/shard_map/ppermute | solution.py:287
  77.0 0.6 ring_2_1.1
  77.5 5.6 %collective-permute-start.8 = (bf16[128,1536]{1,0:T(8,128)(2,1)S(1)}, bf16[128,1536]{1,0:T(8,128)(2,1)S(1)}, u32[]{:S(2)}, u32[]{:S(2)}) collective-permute-start(bf16[128,1536]{1,0:T(8,128)(2,1)S(1)} %ring_2_1.1), channel_id=1, source_target_pairs={{0,896},{64,192},{128,0},{192,320},{256,128},{320,448},{384,256},{... | collective-permute-start | bytes 1179656 | tf_op jit(solution)/shard_map/ppermute | solution.py:287
  83.1 0.0 collective-permute-done.3.refs_6_
  83.1 0.6 ring_2_0.1
  83.7 1.9 %collective-permute-start.4 = (bf16[128,1536]{1,0:T(8,128)(2,1)S(1)}, bf16[128,1536]{1,0:T(8,128)(2,1)S(1)}, u32[]{:S(2)}, u32[]{:S(2)}) collective-permute-start(bf16[128,1536]{1,0:T(8,128)(2,1)S(1)} %ring_2_0.1), channel_id=1, source_target_pairs={{0,128},{64,960},{128,256},{192,64},{256,384},{320,192},{384,512},... | collective-permute-start | bytes 1179656 | tf_op jit(solution)/shard_map/ppermute | solution.py:287
  85.6 6.9 %collective-permute-done.8.refs_6_ = bf16[128,1536]{1,0:T(8,128)(2,1)S(1)} collective-permute-done((bf16[128,1536]{1,0:T(8,128)(2,1)S(1)}, bf16[128,1536]{1,0:T(8,128)(2,1)S(1)}, u32[]{:S(2)}, u32[]{:S(2)}) %collective-permute-start.8) | collective-permute-done | bytes 393248 | tf_op jit(solution)/shard_map/ppermute | solution.py:287
  92.6 0.5 ring_3_1.1
  93.1 0.0 copy-start.2
  93.1 0.0 copy-start.3
  93.1 5.6 %collective-permute-start.9 = (bf16[128,1536]{1,0:T(8,128)(2,1)S(1)}, bf16[128,1536]{1,0:T(8,128)(2,1)S(1)}, u32[]{:S(2)}, u32[]{:S(2)}) collective-permute-start(bf16[128,1536]{1,0:T(8,128)(2,1)S(1)} %ring_3_1.1), channel_id=1, source_target_pairs={{0,896},{64,192},{128,0},{192,320},{256,128},{320,448},{384,256},{... | collective-permute-start | bytes 1179656 | tf_op jit(solution)/shard_map/ppermute | solution.py:287
  98.7 0.0 collective-permute-done.4.refs_6_
  98.8 0.6 ring_3_0.1
  99.3 1.9 %collective-permute-start.5 = (bf16[128,1536]{1,0:T(8,128)(2,1)S(1)}, bf16[128,1536]{1,0:T(8,128)(2,1)S(1)}, u32[]{:S(2)}, u32[]{:S(2)}) collective-permute-start(bf16[128,1536]{1,0:T(8,128)(2,1)S(1)} %ring_3_0.1), channel_id=1, source_target_pairs={{0,128},{64,960},{128,256},{192,64},{256,384},{320,192},{384,512},... | collective-permute-start | bytes 1179656 | tf_op jit(solution)/shard_map/ppermute | solution.py:287
  101.2 0.0 copy-done.2
  101.3 0.0 copy-done.3
  101.3 0.4 spread.1.spread_ref
  101.6 0.6 own.1.own_ref
  102.2 5.2 %collective-permute-done.9.two_ref = bf16[128,1536]{1,0:T(8,128)(2,1)S(1)} collective-permute-done((bf16[128,1536]{1,0:T(8,128)(2,1)S(1)}, bf16[128,1536]{1,0:T(8,128)(2,1)S(1)}, u32[]{:S(2)}, u32[]{:S(2)}) %collective-permute-start.9) | collective-permute-done | bytes 393248 | tf_op jit(solution)/shard_map/ppermute | solution.py:287
  107.4 2.8 %collective-permute-done.5.one_ref = bf16[128,1536]{1,0:T(8,128)(2,1)S(1)} collective-permute-done((bf16[128,1536]{1,0:T(8,128)(2,1)S(1)}, bf16[128,1536]{1,0:T(8,128)(2,1)S(1)}, u32[]{:S(2)}, u32[]{:S(2)}) %collective-permute-start.5) | collective-permute-done | bytes 393248 | tf_op jit(solution)/shard_map/ppermute | solution.py:287
  110.2 1.1 %ring_last.1 = f32[128,1,1536]{2,1,0:T(1,128)} custom-call(f32[128,1536]{1,0:T(8,128)S(1)} %own.1.own_ref, bf16[128,1536]{1,0:T(8,128)(2,1)S(1)} %collective-permute-done.5.one_ref, bf16[128,1536]{1,0:T(8,128)(2,1)S(1)} %collective-permute-done.9.two_ref), custom_call_target="tpu_custom_call" | custom-call | flops 589824 | bytes 2359296 | tf_op jit(solution)/shard_map/ring_last/pallas_call | solution.py:288
  111.3 0.0 all-to-all-done
  111.3 1.1 combine.1
Async XLA Ops:
  2.1 35.0 %all-to-all-start.1 = ((s32[64,1,128]{2,1,0:T(1,128)}), s32[64,1,128]{2,1,0:T(1,128)S(1)}, u32[]{:S(2)}, u32[]{:S(2)}) async-start(s32[64,1,128]{2,1,0:T(1,128)} %get-tuple-element.9), calls=%async_computation.1 | async-start | bytes 65536 | tf_op jit(solution)/shard_map/all_to_all | solution.py:185
  32.4 15.3 %copy-start = (bf16[20,256,128]{2,1,0:T(8,128)(2,1)S(1)}, bf16[20,256,128]{2,1,0:T(8,128)(2,1)}, u32[]{:S(2)}) copy-start(bf16[20,256,128]{2,1,0:T(8,128)(2,1)} %get-tuple-element.11.refs_4_) | copy-start | bytes 3932164
  32.4 20.5 %copy-start.1 = (bf16[8,256,128]{2,1,0:T(8,128)(2,1)S(1)}, bf16[8,256,128]{2,1,0:T(8,128)(2,1)}, u32[]{:S(2)}) copy-start(bf16[8,256,128]{2,1,0:T(8,128)(2,1)} %get-tuple-element.10.refs_2_) | copy-start | bytes 1572868
  37.1 74.2 %all-to-all-start = ((bf16[64,8,1024]{2,1,0:T(8,128)(2,1)}), bf16[64,8,1024]{2,1,0:T(8,128)(2,1)S(1)}, u32[]{:S(2)}, u32[]{:S(2)}) async-start(bf16[64,8,1024]{2,1,0:T(8,128)(2,1)} %bitcast.30), calls=%async_computation | async-start | bytes 2097152 | tf_op jit(solution)/shard_map/all_to_all | solution.py:219
  47.7 5.2 %collective-permute-start.1 = (bf16[20,256,128]{2,1,0:T(8,128)(2,1)S(1)}, bf16[20,256,128]{2,1,0:T(8,128)(2,1)S(1)}, u32[]{:S(2)}, u32[]{:S(2)}) collective-permute-start(bf16[20,256,128]{2,1,0:T(8,128)(2,1)S(1)} %copy-done), channel_id=1, source_target_pairs={{0,64},{64,0},{128,192},{192,128},{256,320},{320,256},{384,448},{4... | collective-permute-start | bytes 3932168 | tf_op jit(solution)/shard_map/ppermute | solution.py:229
  49.6 3.3 %collective-permute-start = (s32[64,128]{1,0:T(8,128)S(1)}, s32[64,128]{1,0:T(8,128)S(1)}, u32[]{:S(2)}, u32[]{:S(2)}) collective-permute-start(s32[64,128]{1,0:T(8,128)S(1)} %bitcast.16), channel_id=1, source_target_pairs={{0,64},{64,0},{128,192},{192,128},{256,320},{320,256},{384,448},{4... | collective-permute-start | bytes 98312 | tf_op jit(solution)/shard_map/ppermute | solution.py:231
  53.3 8.9 %collective-permute-start.6 = (bf16[128,768]{1,0:T(8,128)(2,1)S(1)}, bf16[128,768]{1,0:T(8,128)(2,1)S(1)}, u32[]{:S(2)}, u32[]{:S(2)}) collective-permute-start(bf16[128,768]{1,0:T(8,128)(2,1)S(1)} %ring_0_1.1), channel_id=1, source_target_pairs={{0,896},{64,192},{128,0},{192,320},{256,128},{320,448},{384,256},{... | collective-permute-start | bytes 589832 | tf_op jit(solution)/shard_map/ppermute | solution.py:287
  59.2 9.2 %collective-permute-start.2 = (bf16[128,768]{1,0:T(8,128)(2,1)S(1)}, bf16[128,768]{1,0:T(8,128)(2,1)S(1)}, u32[]{:S(2)}, u32[]{:S(2)}) collective-permute-start(bf16[128,768]{1,0:T(8,128)(2,1)S(1)} %ring_0_0.1), channel_id=1, source_target_pairs={{0,128},{64,960},{128,256},{192,64},{256,384},{320,192},{384,512},... | collective-permute-start | bytes 589832 | tf_op jit(solution)/shard_map/ppermute | solution.py:287
  62.8 14.2 %collective-permute-start.7 = (bf16[128,1536]{1,0:T(8,128)(2,1)S(1)}, bf16[128,1536]{1,0:T(8,128)(2,1)S(1)}, u32[]{:S(2)}, u32[]{:S(2)}) collective-permute-start(bf16[128,1536]{1,0:T(8,128)(2,1)S(1)} %ring_1_1.1), channel_id=1, source_target_pairs={{0,896},{64,192},{128,0},{192,320},{256,128},{320,448},{384,256},{... | collective-permute-start | bytes 1179656 | tf_op jit(solution)/shard_map/ppermute | solution.py:287
  69.0 14.2 %collective-permute-start.3 = (bf16[128,1536]{1,0:T(8,128)(2,1)S(1)}, bf16[128,1536]{1,0:T(8,128)(2,1)S(1)}, u32[]{:S(2)}, u32[]{:S(2)}) collective-permute-start(bf16[128,1536]{1,0:T(8,128)(2,1)S(1)} %ring_1_0.1), channel_id=1, source_target_pairs={{0,128},{64,960},{128,256},{192,64},{256,384},{320,192},{384,512},... | collective-permute-start | bytes 1179656 | tf_op jit(solution)/shard_map/ppermute | solution.py:287
  77.5 15.0 %collective-permute-start.8 = (bf16[128,1536]{1,0:T(8,128)(2,1)S(1)}, bf16[128,1536]{1,0:T(8,128)(2,1)S(1)}, u32[]{:S(2)}, u32[]{:S(2)}) collective-permute-start(bf16[128,1536]{1,0:T(8,128)(2,1)S(1)} %ring_2_1.1), channel_id=1, source_target_pairs={{0,896},{64,192},{128,0},{192,320},{256,128},{320,448},{384,256},{... | collective-permute-start | bytes 1179656 | tf_op jit(solution)/shard_map/ppermute | solution.py:287
  83.7 15.0 %collective-permute-start.4 = (bf16[128,1536]{1,0:T(8,128)(2,1)S(1)}, bf16[128,1536]{1,0:T(8,128)(2,1)S(1)}, u32[]{:S(2)}, u32[]{:S(2)}) collective-permute-start(bf16[128,1536]{1,0:T(8,128)(2,1)S(1)} %ring_2_0.1), channel_id=1, source_target_pairs={{0,128},{64,960},{128,256},{192,64},{256,384},{320,192},{384,512},... | collective-permute-start | bytes 1179656 | tf_op jit(solution)/shard_map/ppermute | solution.py:287
  93.1 8.1 %copy-start.2 = (f32[1,16,8]{1,2,0:T(8,128)S(1)}, f32[1,16,8]{1,2,0:T(8,128)}, u32[]{:S(2)}) copy-start(f32[1,16,8]{1,2,0:T(8,128)} %param.7) | copy-start | bytes 1540
  93.1 8.1 %copy-start.3 = (s32[1,128]{1,0:T(1,128)S(1)}, s32[1,128]{1,0:T(1,128)}, u32[]{:S(2)}) copy-start(s32[1,128]{1,0:T(1,128)} %get-tuple-element.7.tgt_ref) | copy-start | bytes 1540
  93.1 14.3 %collective-permute-start.9 = (bf16[128,1536]{1,0:T(8,128)(2,1)S(1)}, bf16[128,1536]{1,0:T(8,128)(2,1)S(1)}, u32[]{:S(2)}, u32[]{:S(2)}) collective-permute-start(bf16[128,1536]{1,0:T(8,128)(2,1)S(1)} %ring_3_1.1), channel_id=1, source_target_pairs={{0,896},{64,192},{128,0},{192,320},{256,128},{320,448},{384,256},{... | collective-permute-start | bytes 1179656 | tf_op jit(solution)/shard_map/ppermute | solution.py:287
  99.3 10.9 %collective-permute-start.5 = (bf16[128,1536]{1,0:T(8,128)(2,1)S(1)}, bf16[128,1536]{1,0:T(8,128)(2,1)S(1)}, u32[]{:S(2)}, u32[]{:S(2)}) collective-permute-start(bf16[128,1536]{1,0:T(8,128)(2,1)S(1)} %ring_3_0.1), channel_id=1, source_target_pairs={{0,128},{64,960},{128,256},{192,64},{256,384},{320,192},{384,512},... | collective-permute-start | bytes 1179656 | tf_op jit(solution)/shard_map/ppermute | solution.py:287

commit v3 on v2

--- a/solution.py
+++ b/solution.py
@@ -7,6 +7,7 @@
 from jax.sharding import PartitionSpec as P
 
 ROWS_LIMIT = 60 << 20
+CHAINS = 2
 BF16, F32, I32 = jnp.bfloat16, jnp.float32, jnp.int32
 
 
@@ -60,13 +61,15 @@
         tiles = 2 * hidden // part
         for tile in range(tiles):
             trade_ref[tile] = grads_ref[:, tile * part : (tile + 1) * part]
-        second = lax.rem(me_ref[0], 2) == 0
-        for chunk in range(trade_ref.shape[0] - tiles):
-            start = 2 * chunk * part
-            even = rows_ref[:, start : start + part]
-            odd = rows_ref[:, start + part : start + 2 * part]
-            trade_ref[tiles + chunk] = jnp.where(second, odd, even)
-            mine_ref[chunk] = jnp.where(second, even, odd)
+        ring = mine_ref.shape[0]
+        core, chip = lax.rem(me_ref[0], 2), lax.div(me_ref[0], 2)
+        for owner, ref, base in ((core, mine_ref, 0), (1 - core, trade_ref, tiles)):
+            for index in range(ring):
+                k = index // 2 + 1 if index < ring - 2 else (ring // 2, 0)[index - ring + 2]
+                dest = lax.rem(chip + k * (1 - 2 * owner) + ring, ring)
+                row_set = index % 2 if index < ring - 2 else owner
+                start = pl.multiple_of((2 * dest + row_set) * part, part)
+                ref[base + index] = rows_ref[:, pl.ds(start, part)]
 
     grads = grads_ref[...]
     low = dot(grads, wlo_ref[...], 1, 1)
@@ -91,43 +94,59 @@
     return jnp.concatenate([ref[tile] for tile in range(ref.shape[0])], axis=1)
 
 
-def partial_sum(cnt_a, cnt_b, rows_a, rows_b, grads_a, grads_b):
-    slots, part = rows_a.shape[1:]
-    zero = jnp.zeros((), F32)
-    a = jnp.where(live(cnt_a, slots, part), rows_a[0].astype(F32), zero).astype(BF16)
-    b = jnp.where(live(cnt_b, slots, part), rows_b[0].astype(F32), zero).astype(BF16)
-    return dot(a, tiles_of(grads_a), 0, 0) + dot(b, tiles_of(grads_b), 0, 0)
+def masked(cnt_ref, tile, slots, part):
+    return jnp.where(live(cnt_ref, slots, part), tile.astype(F32), jnp.zeros((), F32)).astype(BF16)
+
+
+def tile_sums(cnt_a, cnt_b, rows_a, rows_b, grads_a, grads_b):
+    count, slots, part = rows_a.shape
+    one, two = tiles_of(grads_a), tiles_of(grads_b)
+    return [
+        dot(masked(cnt_a, rows_a[t], slots, part), one, 0, 0)
+        + dot(masked(cnt_b, rows_b[t], slots, part), two, 0, 0)
+        for t in range(count)
+    ]
 
 
 def first_kernel(me_ref, *refs):
-    refs[-1][...] = partial_sum(*refs[:6]).astype(BF16)
-
-
-def second_kernel(side, me_ref, *refs):
-    inc, out_ref = refs[6:]
-    half = inc.shape[1]
-    total = partial_sum(*refs[:6])
-    low, high = total[:, :half], total[:, half:]
-    if side == 0:
-        low = low + inc[...].astype(F32)
-    else:
-        high = high + inc[...].astype(F32)
-    out_ref[:, :half] = low.astype(BF16)
-    out_ref[:, half:] = high.astype(BF16)
+    refs[-1][...] = tile_sums(*refs[:6])[0].astype(BF16)
+
+
+def second_kernel(me_ref, *refs):
+    inc_ref, out_ref = refs[6:]
+    core = lax.rem(me_ref[0], 2)
+    inc = inc_ref[...].astype(F32)
+    for t, total in enumerate(tile_sums(*refs[:6])):
+        out_ref[t] = (total + jnp.where(core == t, inc, jnp.zeros((), F32))).astype(BF16)
 
 
 def middle_kernel(me_ref, *refs):
-    inc, out_ref = refs[6:]
-    out_ref[...] = (partial_sum(*refs[:6]) + inc[...].astype(F32)).astype(BF16)
+    inc_ref, out_ref = refs[6:]
+    for t, total in enumerate(tile_sums(*refs[:6])):
+        out_ref[t] = (total + inc_ref[t].astype(F32)).astype(BF16)
+
+
+def final_kernel(me_ref, *refs):
+    inc_ref, same_ref, cross_ref = refs[6:]
+    low, high = [
+        total + inc_ref[t].astype(F32) for t, total in enumerate(tile_sums(*refs[:6]))
+    ]
+    even = lax.rem(me_ref[0], 2) == 0
+    same_ref[...] = jnp.where(even, low, high).astype(BF16)
+    cross_ref[...] = jnp.where(even, high, low).astype(BF16)
 
 
 def own_kernel(me_ref, *refs):
-    refs[-1][...] = partial_sum(*refs[:6])
-
-
-def last_kernel(replicas, own_ref, one_ref, two_ref, out_ref):
-    total = own_ref[...] + (one_ref[...].astype(F32) + two_ref[...].astype(F32))
-    out_ref[:, 0, :] = total / replicas
+    refs[-1][...] = tile_sums(*refs[:6])[0]
+
+
+def last_kernel(replicas, own_ref, *refs):
+    out_ref = refs[-1]
+    width = refs[0].shape[1]
+    for q in range(CHAINS):
+        cols = slice(q * width, (q + 1) * width)
+        arrived = refs[2 * q][...].astype(F32) + refs[2 * q + 1][...].astype(F32)
+        out_ref[:, 0, cols] = (own_ref[:, cols] + arrived) / replicas
 
 
 def spread_kernel(tgt_ref, w_ref, out_ref):
@@ -149,10 +168,12 @@
 def combine_kernel(spread_ref, recv_ref, out_ref):
     tokens, model = out_ref.shape
     recv = recv_ref[...]
+    width = recv.shape[1]
     for side in range(2):
         both = dot(spread_ref[side], recv, 1, 0)
         out = both[:tokens] + both[tokens:]
-        out_ref[:, side * (model // 2) : (side + 1) * (model // 2)] = out.astype(BF16)
+        start = pl.multiple_of(side * (model // 2) + pl.program_id(0) * width, width)
+        out_ref[:, pl.ds(start, width)] = out.astype(BF16)
 
 
 def shards(ids, weights, rows, gate_up, hidden_grad, expert_weight, interpret=False):
@@ -220,77 +241,70 @@
         sent.reshape(experts, 8, half), "ep", split_axis=0, concat_axis=0, tiled=True
     )
 
-    def neighbour(d, direction):
-        turn = direction if d % 2 == 0 else -direction
-        return ((d // 2 + turn) % ring) * 2 + d % 2
+    def onward(d, cross):
+        core = d % 2
+        return ((d // 2 + 1 - 2 * core) % ring) * 2 + (1 - core if cross else core)
 
     partner = [(d, d ^ 1) for d in range(replicas)]
-    ways = [[(d, neighbour(d, turn)) for d in range(replicas)] for turn in (1, -1)]
+    ways = [[(d, onward(d, cross)) for d in range(replicas)] for cross in (False, True)]
     other = lax.ppermute(trade, "dp", partner)
     counts = counts.reshape(experts, 128)
     other_counts = lax.ppermute(counts, "dp", partner)
 
-    def stage(body, offset, block, incoming, out_shape, out_spec, name):
-        first, count = block
-
-        def chunk(me):
-            turn = offset * (1 - 2 * lax.rem(me[0], 2))
-            return lax.rem(lax.div(me[0], 2) + turn + ring, ring)
-
-        grads = pl.BlockSpec((count, slots, part), lambda i, me: (first, 0, 0))
+    width = wide // CHAINS
+
+    def stage(body, first, count, chain, chains, incoming, out_shapes, name):
+        grads = pl.BlockSpec((tiles // chains, slots, part), lambda i, me: (chain, 0, 0))
         specs = [
             pl.BlockSpec((experts, 128), lambda i, me: (0, 0)),
             pl.BlockSpec((experts, 128), lambda i, me: (0, 0)),
-            pl.BlockSpec((1, slots, part), lambda i, me: (chunk(me), 0, 0)),
-            pl.BlockSpec((1, slots, part), lambda i, me: (tiles + chunk(me), 0, 0)),
+            pl.BlockSpec((count, slots, part), lambda i, me: (first // count, 0, 0)),
+            pl.BlockSpec((count, slots, part), lambda i, me: ((tiles + first) // count, 0, 0)),
             grads,
             grads,
         ]
-        specs += [pl.BlockSpec(a.shape, lambda i, me: (0, 0)) for a in incoming]
+        block = lambda a: pl.BlockSpec(a.shape, lambda i, me: (0,) * len(a.shape))
         return call(
             body,
             grid_spec=pltpu.PrefetchScalarGridSpec(
-                num_scalar_prefetch=1, grid=(1,), in_specs=specs, out_specs=out_spec
+                num_scalar_prefetch=1,
+                grid=(1,),
+                in_specs=specs + [block(a) for a in incoming],
+                out_specs=[block(a) for a in out_shapes],
             ),
-            out_shape=out_shape,
+            out_shape=out_shapes,
             cost_estimate=cost(
-                4 * part * slots * count * part, 4 * slots * count * part + 4 * part * wide
+                4 * count * part * slots * wide // chains,
+                4 * slots * wide // chains + 4 * part * wide,
             ),
             name=name,
         )(me, counts, other_counts, mine, other, trade, other, *incoming)
 
-    def flat(columns):
-        return sds((part, columns), BF16), pl.BlockSpec((part, columns), lambda i, me: (0, 0))
-
-    own = stage(
-        own_kernel,
-        0,
-        (0, tiles),
-        [],
-        sds((part, wide), F32),
-        pl.BlockSpec((part, wide), lambda i, me: (0, 0)),
-        "own",
-    )
-    state = [None, None]
+    own = stage(own_kernel, ring - 1, 1, 0, 1, [], [sds((part, wide), F32)], "own")
+    one, two = sds((part, width), BF16), sds((2, part, width), BF16)
+    state = [[]] * CHAINS
     for step in range(ring // 2):
-        k = ring // 2 - step
-        for side in range(2):
-            if step == 0:
-                block = (side, tiles // 2)
-                send = stage(first_kernel, k, block, [], *flat(wide // 2), f"ring_{step}_{side}")
-            else:
-                body = functools.partial(second_kernel, side) if step == 1 else middle_kernel
-                offset = k if side == 0 else -k
-                send = stage(
-                    body, offset, (0, tiles), [state[side]], *flat(wide), f"ring_{step}_{side}"
-                )
-            state[side] = lax.ppermute(send, "dp", ways[side])
+        first, count = (ring - 2, 1) if step == 0 else (ring - 2 - 2 * step, 2)
+        final = step == ring // 2 - 1
+        body = (first_kernel, second_kernel, middle_kernel)[min(step, 2)]
+        for chain in range(CHAINS):
+            sends = stage(
+                final_kernel if final else body,
+                first,
+                count,
+                chain,
+                CHAINS,
+                state[chain],
+                [one, one] if final else [one if step == 0 else two],
+                f"ring_{step}_{chain}",
+            )
+            state[chain] = [lax.ppermute(a, "dp", way) for a, way in zip(sends, ways)]
     weight_grad = call(
         functools.partial(last_kernel, replicas),
         out_shape=sds((part, 1, wide), F32),
         cost_estimate=cost(3 * part * wide, 12 * part * wide),
         name="ring_last",
-    )(own, *state)
+    )(own[0], *state[0], *state[1])
 
     spread = call(
         spread_kernel,
@@ -300,6 +314,12 @@
     )(target, weights.reshape(tokens, chosen).T)
     input_grad = call(
         combine_kernel,
+        grid=(steps,),
+        in_specs=[
+            pl.BlockSpec((2, 2 * tokens, experts * 8), lambda i: (0, 0, 0)),
+            pl.BlockSpec((experts * 8, tile), lambda i: (0, i)),
+        ],
+        out_specs=pl.BlockSpec((tokens, model), lambda i: (0, 0)),
         out_shape=sds((tokens, model), BF16),
         cost_estimate=cost(8 * tokens * experts * 8 * model, 2 * slots * model),
         name="combine",

time: 113 us -> 108 us (0.956)
  the two profiles are of different devices: /device:TPU:6 before, /device:TPU:1 now
where the time goes in v3:
time: 108 us; the launch traced here: 107 us
  starting transfers between devices  75.6 us (70%)
  Pallas kernels  17.2 us (16%)
  waiting for transfers between devices  13.5 us (12%)
    ppermute x10, starting transfers between devices, shards(): state[chain] = [lax.ppermute(a, 'dp', way) for a, way in zip(sends, ways)]  38.3 us
    all_to_all x1, starting transfers between devices, shards(): lax.all_to_all(counts, 'ep', split_axis=0, concat_axis=0, tiled=True)  22.8 us
    all_to_all x1, starting transfers between devices, shards(): lax.all_to_all(sent.reshape(experts, 8, half), 'ep', split_axis=0, concat...  9.13 us
    pallas_call x1, Pallas kernels, shards(): call(rows_kernel, limit=ROWS_LIMIT, grid_spec=pltpu.PrefetchScalarGridSpe...  7.64 us
    ppermute x10, waiting for transfers between devices, shards(): state[chain] = [lax.ppermute(a, 'dp', way) for a, way in zip(sends, ways)]  6.72 us
    all_to_all x1, waiting for transfers between devices, shards(): lax.all_to_all(counts, 'ep', split_axis=0, concat_axis=0, tiled=True)  5.59 us
    pallas_call x9, Pallas kernels, stage(): call(body, grid_spec=pltpu.PrefetchScalarGridSpec(num_scalar_prefetch=1,...  4.91 us
    ppermute x1, starting transfers between devices, shards(): other = lax.ppermute(trade, 'dp', partner)  3.42 us
  transfers between devices with their start and end apart: 14, of which 6 were waited for; matrix products, arithmetic and copies ran while one was open for 0% of the time, Pallas kernels for 13%

profile of v3, /device:TPU:1, one launch (start us, length us, event | category | flops | bytes accessed | tf_op | source)
XLA Modules:
  0.0 107.1 jit_solution(11780883030701289953)
XLA Ops:
  0.6 1.5 %route.1 = (s32[64,1,128]{2,1,0:T(1,128)}, s32[1,128]{1,0:T(1,128)}) custom-call(s32[8,16]{1,0:T(8,128)} %bitcast.34), custom_call_target="tpu_custom_call" | custom-call | tf_op jit(solution)/shard_map/route/pallas_call | solution.py:200
  2.1 22.8 %all-to-all-start.1 = ((s32[64,1,128]{2,1,0:T(1,128)}), s32[64,1,128]{2,1,0:T(1,128)S(1)}, u32[]{:S(2)}, u32[]{:S(2)}) async-start(s32[64,1,128]{2,1,0:T(1,128)} %get-tuple-element.13), calls=%async_computation.1 | async-start | bytes 65536 | tf_op jit(solution)/shard_map/all_to_all | solution.py:206
  24.9 7.6 %rows.1 = (bf16[20,256,128]{2,1,0:T(8,128)(2,1)}, bf16[8,256,128]{2,1,0:T(8,128)(2,1)}, bf16[32,2,8,1024]{3,2,1,0:T(8,128)(2,1)}) custom-call(s32[1]{0:T(128)} %bitcast.4.me_ref, bf16[256,1536]{1,0:T(8,128)(2,1)} %bitcast.31, bf16[256,768]{1,0:T(8,128)(2,1)} %bitcast.32, bf16[256,2048]{1,0:T(8,128)(2,1)} %bitcast.29, bf16[2048,1536]{1,0:T(8,128)(2,1)} %bitcast.27, ...), custom_call_target="tpu_custom_call" | custom-call | flops 1610612736 | bytes 9437184 | tf_op jit(solution)/shard_map/rows/pallas_call | solution.py:212
  32.6 5.6 %all-to-all-done.1 = s32[64,1,128]{2,1,0:T(1,128)S(1)} async-done(((s32[64,1,128]{2,1,0:T(1,128)}), s32[64,1,128]{2,1,0:T(1,128)S(1)}, u32[]{:S(2)}, u32[]{:S(2)}) %all-to-all-start.1) | async-done | bytes 32800 | tf_op jit(solution)/shard_map/all_to_all | solution.py:206
  38.2 9.1 %all-to-all-start = ((bf16[64,8,1024]{2,1,0:T(8,128)(2,1)}), bf16[64,8,1024]{2,1,0:T(8,128)(2,1)S(1)}, u32[]{:S(2)}, u32[]{:S(2)}) async-start(bf16[64,8,1024]{2,1,0:T(8,128)(2,1)} %bitcast.30), calls=%async_computation | async-start | bytes 2097152 | tf_op jit(solution)/shard_map/all_to_all | solution.py:240
  47.3 0.0 copy-done
  47.3 3.4 %collective-permute-start.1 = (bf16[20,256,128]{2,1,0:T(8,128)(2,1)S(1)}, bf16[20,256,128]{2,1,0:T(8,128)(2,1)S(1)}, u32[]{:S(2)}, u32[]{:S(2)}) collective-permute-start(bf16[20,256,128]{2,1,0:T(8,128)(2,1)S(1)} %copy-done), channel_id=1, source_target_pairs={{0,64},{64,0},{128,192},{192,128},{256,320},{320,256},{384,448},{4... | collective-permute-start | bytes 3932168 | tf_op jit(solution)/shard_map/ppermute | solution.py:250
  50.7 1.9 %collective-permute-start = (s32[64,128]{1,0:T(8,128)S(1)}, s32[64,128]{1,0:T(8,128)S(1)}, u32[]{:S(2)}, u32[]{:S(2)}) collective-permute-start(s32[64,128]{1,0:T(8,128)S(1)} %bitcast.16), channel_id=1, source_target_pairs={{0,64},{64,0},{128,192},{192,128},{256,320},{320,256},{384,448},{4... | collective-permute-start | bytes 98312 | tf_op jit(solution)/shard_map/ppermute | solution.py:252
  52.7 1.2 %collective-permute-done.refs_1_ = s32[64,128]{1,0:T(8,128)S(1)} collective-permute-done((s32[64,128]{1,0:T(8,128)S(1)}, s32[64,128]{1,0:T(8,128)S(1)}, u32[]{:S(2)}, u32[]{:S(2)}) %collective-permute-start) | collective-permute-done | bytes 32800 | tf_op jit(solution)/shard_map/ppermute | solution.py:252
  53.8 0.0 collective-permute-done.1.refs_3_.refs_5_
  53.8 0.0 copy-done.1
  53.8 0.4 ring_0_1.1
  54.3 5.1 %collective-permute-start.7 = (bf16[128,768]{1,0:T(8,128)(2,1)S(1)}, bf16[128,768]{1,0:T(8,128)(2,1)S(1)}, u32[]{:S(2)}, u32[]{:S(2)}) collective-permute-start(bf16[128,768]{1,0:T(8,128)(2,1)S(1)} %ring_0_1.1), channel_id=1, source_target_pairs={{0,128},{64,960},{128,256},{192,64},{256,384},{320,192},{384,512},... | collective-permute-start | bytes 589832 | tf_op jit(solution)/shard_map/ppermute | solution.py:301
  59.4 0.4 ring_0_0.1
  59.8 3.0 %collective-permute-start.2 = (bf16[128,768]{1,0:T(8,128)(2,1)S(1)}, bf16[128,768]{1,0:T(8,128)(2,1)S(1)}, u32[]{:S(2)}, u32[]{:S(2)}) collective-permute-start(bf16[128,768]{1,0:T(8,128)(2,1)S(1)} %ring_0_0.1), channel_id=1, source_target_pairs={{0,128},{64,960},{128,256},{192,64},{256,384},{320,192},{384,512},... | collective-permute-start | bytes 589832 | tf_op jit(solution)/shard_map/ppermute | solution.py:301
  62.8 0.0 collective-permute-done.7.refs_6_
  62.8 0.6 ring_1_1.1
  63.4 4.5 %collective-permute-start.8 = (bf16[2,128,768]{2,1,0:T(8,128)(2,1)S(1)}, bf16[2,128,768]{2,1,0:T(8,128)(2,1)S(1)}, u32[]{:S(2)}, u32[]{:S(2)}) collective-permute-start(bf16[2,128,768]{2,1,0:T(8,128)(2,1)S(1)} %ring_1_1.1), channel_id=1, source_target_pairs={{0,128},{64,960},{128,256},{192,64},{256,384},{320,192},{384,512},... | collective-permute-start | bytes 1179656 | tf_op jit(solution)/shard_map/ppermute | solution.py:301
  67.9 0.0 collective-permute-done.2.refs_6_
  67.9 0.6 ring_1_0.1
  68.5 2.9 %collective-permute-start.3 = (bf16[2,128,768]{2,1,0:T(8,128)(2,1)S(1)}, bf16[2,128,768]{2,1,0:T(8,128)(2,1)S(1)}, u32[]{:S(2)}, u32[]{:S(2)}) collective-permute-start(bf16[2,128,768]{2,1,0:T(8,128)(2,1)S(1)} %ring_1_0.1), channel_id=1, source_target_pairs={{0,128},{64,960},{128,256},{192,64},{256,384},{320,192},{384,512},... | collective-permute-start | bytes 1179656 | tf_op jit(solution)/shard_map/ppermute | solution.py:301
  71.3 1.3 %collective-permute-done.8.refs_6_ = bf16[2,128,768]{2,1,0:T(8,128)(2,1)S(1)} collective-permute-done((bf16[2,128,768]{2,1,0:T(8,128)(2,1)S(1)}, bf16[2,128,768]{2,1,0:T(8,128)(2,1)S(1)}, u32[]{:S(2)}, u32[]{:S(2)}) %collective-permute-start.8) | collective-permute-done | bytes 393248 | tf_op jit(solution)/shard_map/ppermute | solution.py:301
  72.6 0.6 ring_2_1.1
  73.1 5.3 %collective-permute-start.9 = (bf16[2,128,768]{2,1,0:T(8,128)(2,1)S(1)}, bf16[2,128,768]{2,1,0:T(8,128)(2,1)S(1)}, u32[]{:S(2)}, u32[]{:S(2)}) collective-permute-start(bf16[2,128,768]{2,1,0:T(8,128)(2,1)S(1)} %ring_2_1.1), channel_id=1, source_target_pairs={{0,128},{64,960},{128,256},{192,64},{256,384},{320,192},{384,512},... | collective-permute-start | bytes 1179656 | tf_op jit(solution)/shard_map/ppermute | solution.py:301
  78.5 0.0 collective-permute-done.3.refs_6_
  78.5 0.6 ring_2_0.1
  79.1 3.6 %collective-permute-start.4 = (bf16[2,128,768]{2,1,0:T(8,128)(2,1)S(1)}, bf16[2,128,768]{2,1,0:T(8,128)(2,1)S(1)}, u32[]{:S(2)}, u32[]{:S(2)}) collective-permute-start(bf16[2,128,768]{2,1,0:T(8,128)(2,1)S(1)} %ring_2_0.1), channel_id=1, source_target_pairs={{0,128},{64,960},{128,256},{192,64},{256,384},{320,192},{384,512},... | collective-permute-start | bytes 1179656 | tf_op jit(solution)/shard_map/ppermute | solution.py:301
  82.7 0.5 collective-permute-done.9.refs_6_
  83.2 0.6 ring_3_1.1
  83.8 5.3 %collective-permute-start.10 = (bf16[128,768]{1,0:T(8,128)(2,1)S(1)}, bf16[128,768]{1,0:T(8,128)(2,1)S(1)}, u32[]{:S(2)}, u32[]{:S(2)}) collective-permute-start(bf16[128,768]{1,0:T(8,128)(2,1)S(1)} %get-tuple-element.18), channel_id=1, source_target_pairs={{0,128},{64,960},{128,256},{192,64},{256,384},{320,192},{384,512},... | collective-permute-start | bytes 589832 | tf_op jit(solution)/shard_map/ppermute | solution.py:301
  89.1 0.0 copy-start.2
  89.1 0.0 copy-start.3
  89.1 4.5 %collective-permute-start.11 = (bf16[128,768]{1,0:T(8,128)(2,1)S(1)}, bf16[128,768]{1,0:T(8,128)(2,1)S(1)}, u32[]{:S(2)}, u32[]{:S(2)}) collective-permute-start(bf16[128,768]{1,0:T(8,128)(2,1)S(1)} %get-tuple-element.19), channel_id=1, source_target_pairs={{0,192},{64,896},{128,320},{192,0},{256,448},{320,128},{384,576},{... | collective-permute-start | bytes 589832 | tf_op jit(solution)/shard_map/ppermute | solution.py:301
  93.7 0.0 collective-permute-done.4.refs_6_
  93.7 0.6 ring_3_0.1
  94.3 1.9 %collective-permute-start.5 = (bf16[128,768]{1,0:T(8,128)(2,1)S(1)}, bf16[128,768]{1,0:T(8,128)(2,1)S(1)}, u32[]{:S(2)}, u32[]{:S(2)}) collective-permute-start(bf16[128,768]{1,0:T(8,128)(2,1)S(1)} %get-tuple-element.16), channel_id=1, source_target_pairs={{0,128},{64,960},{128,256},{192,64},{256,384},{320,192},{384,512},... | collective-permute-start | bytes 589832 | tf_op jit(solution)/shard_map/ppermute | solution.py:301
  96.2 2.2 %collective-permute-start.6 = (bf16[128,768]{1,0:T(8,128)(2,1)S(1)}, bf16[128,768]{1,0:T(8,128)(2,1)S(1)}, u32[]{:S(2)}, u32[]{:S(2)}) collective-permute-start(bf16[128,768]{1,0:T(8,128)(2,1)S(1)} %get-tuple-element.17), channel_id=1, source_target_pairs={{0,192},{64,896},{128,320},{192,0},{256,448},{320,128},{384,576},{... | collective-permute-start | bytes 589832 | tf_op jit(solution)/shard_map/ppermute | solution.py:301
  98.5 0.0 copy-done.2
  98.5 0.0 copy-done.3
  98.5 0.4 spread.1.spread_ref
  98.9 0.6 own.1.own_ref
  99.4 0.0 collective-permute-done.10.refs_2_
  99.4 0.0 collective-permute-done.11.refs_3_
  99.4 1.5 %collective-permute-done.5.refs_0_ = bf16[128,768]{1,0:T(8,128)(2,1)S(1)} collective-permute-done((bf16[128,768]{1,0:T(8,128)(2,1)S(1)}, bf16[128,768]{1,0:T(8,128)(2,1)S(1)}, u32[]{:S(2)}, u32[]{:S(2)}) %collective-permute-start.5) | collective-permute-done | bytes 196640 | tf_op jit(solution)/shard_map/ppermute | solution.py:301
  101.0 3.4 %collective-permute-done.6.refs_1_ = bf16[128,768]{1,0:T(8,128)(2,1)S(1)} collective-permute-done((bf16[128,768]{1,0:T(8,128)(2,1)S(1)}, bf16[128,768]{1,0:T(8,128)(2,1)S(1)}, u32[]{:S(2)}, u32[]{:S(2)}) %collective-permute-start.6) | collective-permute-done | bytes 196640 | tf_op jit(solution)/shard_map/ppermute | solution.py:301
  104.4 1.2 %ring_last.1 = f32[128,1,1536]{2,1,0:T(1,128)} custom-call(f32[128,1536]{1,0:T(8,128)S(1)} %own.1.own_ref, bf16[128,768]{1,0:T(8,128)(2,1)S(1)} %collective-permute-done.5.refs_0_, bf16[128,768]{1,0:T(8,128)(2,1)S(1)} %collective-permute-done.6.refs_1_, bf16[128,768]{1,0:T(8,128)(2,1)S(1)} %collective-permute-done.10.refs_2_, ...), custom_call_target="tpu_custom_call" | custom-call | flops 589824 | bytes 2359296 | tf_op jit(solution)/shard_map/ring_last/pallas_call | solution.py:302
  105.6 0.0 all-to-all-done
  105.6 1.6 %combine.1 = bf16[16,2048]{1,0:T(8,128)(2,1)} custom-call(bf16[2,32,512]{2,1,0:T(8,128)(2,1)S(1)} %spread.1.spread_ref, bf16[512,1024]{1,0:T(8,128)(2,1)S(1)} %bitcast.15), custom_call_target="tpu_custom_call" | custom-call | flops 134217728 | bytes 1048576 | tf_op jit(solution)/shard_map/combine/pallas_call | solution.py:315
  (2 shorter events, 0.0 us)
Async XLA Ops:
  2.1 36.0 %all-to-all-start.1 = ((s32[64,1,128]{2,1,0:T(1,128)}), s32[64,1,128]{2,1,0:T(1,128)S(1)}, u32[]{:S(2)}, u32[]{:S(2)}) async-start(s32[64,1,128]{2,1,0:T(1,128)} %get-tuple-element.13), calls=%async_computation.1 | async-start | bytes 65536 | tf_op jit(solution)/shard_map/all_to_all | solution.py:206
  32.6 14.7 %copy-start = (bf16[20,256,128]{2,1,0:T(8,128)(2,1)S(1)}, bf16[20,256,128]{2,1,0:T(8,128)(2,1)}, u32[]{:S(2)}) copy-start(bf16[20,256,128]{2,1,0:T(8,128)(2,1)} %get-tuple-element.15.refs_4_) | copy-start | bytes 3932164
  32.6 21.3 %copy-start.1 = (bf16[8,256,128]{2,1,0:T(8,128)(2,1)S(1)}, bf16[8,256,128]{2,1,0:T(8,128)(2,1)}, u32[]{:S(2)}) copy-start(bf16[8,256,128]{2,1,0:T(8,128)(2,1)} %get-tuple-element.14.refs_2_) | copy-start | bytes 1572868
  38.2 67.4 %all-to-all-start = ((bf16[64,8,1024]{2,1,0:T(8,128)(2,1)}), bf16[64,8,1024]{2,1,0:T(8,128)(2,1)S(1)}, u32[]{:S(2)}, u32[]{:S(2)}) async-start(bf16[64,8,1024]{2,1,0:T(8,128)(2,1)} %bitcast.30), calls=%async_computation | async-start | bytes 2097152 | tf_op jit(solution)/shard_map/all_to_all | solution.py:240
  47.3 6.5 %collective-permute-start.1 = (bf16[20,256,128]{2,1,0:T(8,128)(2,1)S(1)}, bf16[20,256,128]{2,1,0:T(8,128)(2,1)S(1)}, u32[]{:S(2)}, u32[]{:S(2)}) collective-permute-start(bf16[20,256,128]{2,1,0:T(8,128)(2,1)S(1)} %copy-done), channel_id=1, source_target_pairs={{0,64},{64,0},{128,192},{192,128},{256,320},{320,256},{384,448},{4... | collective-permute-start | bytes 3932168 | tf_op jit(solution)/shard_map/ppermute | solution.py:250
  50.7 3.1 %collective-permute-start = (s32[64,128]{1,0:T(8,128)S(1)}, s32[64,128]{1,0:T(8,128)S(1)}, u32[]{:S(2)}, u32[]{:S(2)}) collective-permute-start(s32[64,128]{1,0:T(8,128)S(1)} %bitcast.16), channel_id=1, source_target_pairs={{0,64},{64,0},{128,192},{192,128},{256,320},{320,256},{384,448},{4... | collective-permute-start | bytes 98312 | tf_op jit(solution)/shard_map/ppermute | solution.py:252
  54.3 8.5 %collective-permute-start.7 = (bf16[128,768]{1,0:T(8,128)(2,1)S(1)}, bf16[128,768]{1,0:T(8,128)(2,1)S(1)}, u32[]{:S(2)}, u32[]{:S(2)}) collective-permute-start(bf16[128,768]{1,0:T(8,128)(2,1)S(1)} %ring_0_1.1), channel_id=1, source_target_pairs={{0,128},{64,960},{128,256},{192,64},{256,384},{320,192},{384,512},... | collective-permute-start | bytes 589832 | tf_op jit(solution)/shard_map/ppermute | solution.py:301
  59.8 8.0 %collective-permute-start.2 = (bf16[128,768]{1,0:T(8,128)(2,1)S(1)}, bf16[128,768]{1,0:T(8,128)(2,1)S(1)}, u32[]{:S(2)}, u32[]{:S(2)}) collective-permute-start(bf16[128,768]{1,0:T(8,128)(2,1)S(1)} %ring_0_0.1), channel_id=1, source_target_pairs={{0,128},{64,960},{128,256},{192,64},{256,384},{320,192},{384,512},... | collective-permute-start | bytes 589832 | tf_op jit(solution)/shard_map/ppermute | solution.py:301
  63.4 9.2 %collective-permute-start.8 = (bf16[2,128,768]{2,1,0:T(8,128)(2,1)S(1)}, bf16[2,128,768]{2,1,0:T(8,128)(2,1)S(1)}, u32[]{:S(2)}, u32[]{:S(2)}) collective-permute-start(bf16[2,128,768]{2,1,0:T(8,128)(2,1)S(1)} %ring_1_1.1), channel_id=1, source_target_pairs={{0,128},{64,960},{128,256},{192,64},{256,384},{320,192},{384,512},... | collective-permute-start | bytes 1179656 | tf_op jit(solution)/shard_map/ppermute | solution.py:301
  68.5 10.0 %collective-permute-start.3 = (bf16[2,128,768]{2,1,0:T(8,128)(2,1)S(1)}, bf16[2,128,768]{2,1,0:T(8,128)(2,1)S(1)}, u32[]{:S(2)}, u32[]{:S(2)}) collective-permute-start(bf16[2,128,768]{2,1,0:T(8,128)(2,1)S(1)} %ring_1_0.1), channel_id=1, source_target_pairs={{0,128},{64,960},{128,256},{192,64},{256,384},{320,192},{384,512},... | collective-permute-start | bytes 1179656 | tf_op jit(solution)/shard_map/ppermute | solution.py:301
  73.1 10.0 %collective-permute-start.9 = (bf16[2,128,768]{2,1,0:T(8,128)(2,1)S(1)}, bf16[2,128,768]{2,1,0:T(8,128)(2,1)S(1)}, u32[]{:S(2)}, u32[]{:S(2)}) collective-permute-start(bf16[2,128,768]{2,1,0:T(8,128)(2,1)S(1)} %ring_2_1.1), channel_id=1, source_target_pairs={{0,128},{64,960},{128,256},{192,64},{256,384},{320,192},{384,512},... | collective-permute-start | bytes 1179656 | tf_op jit(solution)/shard_map/ppermute | solution.py:301
  79.1 14.6 %collective-permute-start.4 = (bf16[2,128,768]{2,1,0:T(8,128)(2,1)S(1)}, bf16[2,128,768]{2,1,0:T(8,128)(2,1)S(1)}, u32[]{:S(2)}, u32[]{:S(2)}) collective-permute-start(bf16[2,128,768]{2,1,0:T(8,128)(2,1)S(1)} %ring_2_0.1), channel_id=1, source_target_pairs={{0,128},{64,960},{128,256},{192,64},{256,384},{320,192},{384,512},... | collective-permute-start | bytes 1179656 | tf_op jit(solution)/shard_map/ppermute | solution.py:301
  83.8 15.7 %collective-permute-start.10 = (bf16[128,768]{1,0:T(8,128)(2,1)S(1)}, bf16[128,768]{1,0:T(8,128)(2,1)S(1)}, u32[]{:S(2)}, u32[]{:S(2)}) collective-permute-start(bf16[128,768]{1,0:T(8,128)(2,1)S(1)} %get-tuple-element.18), channel_id=1, source_target_pairs={{0,128},{64,960},{128,256},{192,64},{256,384},{320,192},{384,512},... | collective-permute-start | bytes 589832 | tf_op jit(solution)/shard_map/ppermute | solution.py:301
  89.1 9.4 %copy-start.2 = (f32[1,16,8]{1,2,0:T(8,128)S(1)}, f32[1,16,8]{1,2,0:T(8,128)}, u32[]{:S(2)}) copy-start(f32[1,16,8]{1,2,0:T(8,128)} %param.7) | copy-start | bytes 1540
  89.1 9.4 %copy-start.3 = (s32[1,128]{1,0:T(1,128)S(1)}, s32[1,128]{1,0:T(1,128)}, u32[]{:S(2)}) copy-start(s32[1,128]{1,0:T(1,128)} %get-tuple-element.11.tgt_ref) | copy-start | bytes 1540
  89.1 10.3 %collective-permute-start.11 = (bf16[128,768]{1,0:T(8,128)(2,1)S(1)}, bf16[128,768]{1,0:T(8,128)(2,1)S(1)}, u32[]{:S(2)}, u32[]{:S(2)}) collective-permute-start(bf16[128,768]{1,0:T(8,128)(2,1)S(1)} %get-tuple-element.19), channel_id=1, source_target_pairs={{0,192},{64,896},{128,320},{192,0},{256,448},{320,128},{384,576},{... | collective-permute-start | bytes 589832 | tf_op jit(solution)/shard_map/ppermute | solution.py:301
  94.3 6.7 %collective-permute-start.5 = (bf16[128,768]{1,0:T(8,128)(2,1)S(1)}, bf16[128,768]{1,0:T(8,128)(2,1)S(1)}, u32[]{:S(2)}, u32[]{:S(2)}) collective-permute-start(bf16[128,768]{1,0:T(8,128)(2,1)S(1)} %get-tuple-element.16), channel_id=1, source_target_pairs={{0,128},{64,960},{128,256},{192,64},{256,384},{320,192},{384,512},... | collective-permute-start | bytes 589832 | tf_op jit(solution)/shard_map/ppermute | solution.py:301
  96.2 8.2 %collective-permute-start.6 = (bf16[128,768]{1,0:T(8,128)(2,1)S(1)}, bf16[128,768]{1,0:T(8,128)(2,1)S(1)}, u32[]{:S(2)}, u32[]{:S(2)}) collective-permute-start(bf16[128,768]{1,0:T(8,128)(2,1)S(1)} %get-tuple-element.17), channel_id=1, source_target_pairs={{0,192},{64,896},{128,320},{192,0},{256,448},{320,128},{384,576},{... | collective-permute-start | bytes 589832 | tf_op jit(solution)/shard_map/ppermute | solution.py:301

commit v4 on v3

--- a/solution.py
+++ b/solution.py
@@ -168,12 +168,10 @@
 def combine_kernel(spread_ref, recv_ref, out_ref):
     tokens, model = out_ref.shape
     recv = recv_ref[...]
-    width = recv.shape[1]
     for side in range(2):
         both = dot(spread_ref[side], recv, 1, 0)
         out = both[:tokens] + both[tokens:]
-        start = pl.multiple_of(side * (model // 2) + pl.program_id(0) * width, width)
-        out_ref[:, pl.ds(start, width)] = out.astype(BF16)
+        out_ref[:, side * (model // 2) : (side + 1) * (model // 2)] = out.astype(BF16)
 
 
 def shards(ids, weights, rows, gate_up, hidden_grad, expert_weight, interpret=False):
@@ -314,12 +312,6 @@
     )(target, weights.reshape(tokens, chosen).T)
     input_grad = call(
         combine_kernel,
-        grid=(steps,),
-        in_specs=[
-            pl.BlockSpec((2, 2 * tokens, experts * 8), lambda i: (0, 0, 0)),
-            pl.BlockSpec((experts * 8, tile), lambda i: (0, i)),
-        ],
-        out_specs=pl.BlockSpec((tokens, model), lambda i: (0, 0)),
         out_shape=sds((tokens, model), BF16),
         cost_estimate=cost(8 * tokens * experts * 8 * model, 2 * slots * model),
         name="combine",

time: 108 us -> 107 us (level)
  no operation moved by 1% of the time
where the time goes in v4:
time: 107 us
  starting transfers between devices  75.6 us (71%)
  Pallas kernels  16.7 us (16%)
  waiting for transfers between devices  13.5 us (13%)
    ppermute x10, starting transfers between devices, shards(): state[chain] = [lax.ppermute(a, 'dp', way) for a, way in zip(sends, ways)]  38.3 us
    all_to_all x1, starting transfers between devices, shards(): lax.all_to_all(counts, 'ep', split_axis=0, concat_axis=0, tiled=True)  22.8 us
    all_to_all x1, starting transfers between devices, shards(): lax.all_to_all(sent.reshape(experts, 8, half), 'ep', split_axis=0, concat...  9.13 us
    pallas_call x1, Pallas kernels, shards(): call(rows_kernel, limit=ROWS_LIMIT, grid_spec=pltpu.PrefetchScalarGridSpe...  7.64 us
    ppermute x10, waiting for transfers between devices, shards(): state[chain] = [lax.ppermute(a, 'dp', way) for a, way in zip(sends, ways)]  6.72 us
    all_to_all x1, waiting for transfers between devices, shards(): lax.all_to_all(counts, 'ep', split_axis=0, concat_axis=0, tiled=True)  5.59 us
    pallas_call x9, Pallas kernels, stage(): call(body, grid_spec=pltpu.PrefetchScalarGridSpec(num_scalar_prefetch=1,...  4.91 us
    ppermute x1, starting transfers between devices, shards(): other = lax.ppermute(trade, 'dp', partner)  3.42 us
  transfers between devices with their start and end apart: 14, of which 6 were waited for; matrix products, arithmetic and copies ran while one was open for 0% of the time, Pallas kernels for 13%

profile of v4, /device:TPU:1, one launch (start us, length us, event | category | flops | bytes accessed | tf_op | source)
XLA Modules:
  0.0 106.7 jit_solution(12442629674175321013)
XLA Ops:
  0.6 1.5 %route.1 = (s32[64,1,128]{2,1,0:T(1,128)}, s32[1,128]{1,0:T(1,128)}) custom-call(s32[8,16]{1,0:T(8,128)} %bitcast.34), custom_call_target="tpu_custom_call" | custom-call | tf_op jit(solution)/shard_map/route/pallas_call | solution.py:198
  2.1 22.8 %all-to-all-start.1 = ((s32[64,1,128]{2,1,0:T(1,128)}), s32[64,1,128]{2,1,0:T(1,128)S(1)}, u32[]{:S(2)}, u32[]{:S(2)}) async-start(s32[64,1,128]{2,1,0:T(1,128)} %get-tuple-element.13), calls=%async_computation.1 | async-start | bytes 65536 | tf_op jit(solution)/shard_map/all_to_all | solution.py:204
  24.9 7.6 %rows.1 = (bf16[20,256,128]{2,1,0:T(8,128)(2,1)}, bf16[8,256,128]{2,1,0:T(8,128)(2,1)}, bf16[32,2,8,1024]{3,2,1,0:T(8,128)(2,1)}) custom-call(s32[1]{0:T(128)} %bitcast.4.me_ref, bf16[256,1536]{1,0:T(8,128)(2,1)} %bitcast.31, bf16[256,768]{1,0:T(8,128)(2,1)} %bitcast.32, bf16[256,2048]{1,0:T(8,128)(2,1)} %bitcast.29, bf16[2048,1536]{1,0:T(8,128)(2,1)} %bitcast.27, ...), custom_call_target="tpu_custom_call" | custom-call | flops 1610612736 | bytes 9437184 | tf_op jit(solution)/shard_map/rows/pallas_call | solution.py:210
  32.6 5.6 %all-to-all-done.1 = s32[64,1,128]{2,1,0:T(1,128)S(1)} async-done(((s32[64,1,128]{2,1,0:T(1,128)}), s32[64,1,128]{2,1,0:T(1,128)S(1)}, u32[]{:S(2)}, u32[]{:S(2)}) %all-to-all-start.1) | async-done | bytes 32800 | tf_op jit(solution)/shard_map/all_to_all | solution.py:204
  38.2 9.1 %all-to-all-start = ((bf16[64,8,1024]{2,1,0:T(8,128)(2,1)}), bf16[64,8,1024]{2,1,0:T(8,128)(2,1)S(1)}, u32[]{:S(2)}, u32[]{:S(2)}) async-start(bf16[64,8,1024]{2,1,0:T(8,128)(2,1)} %bitcast.30), calls=%async_computation | async-start | bytes 2097152 | tf_op jit(solution)/shard_map/all_to_all | solution.py:238
  47.3 0.0 copy-done
  47.3 3.4 %collective-permute-start.1 = (bf16[20,256,128]{2,1,0:T(8,128)(2,1)S(1)}, bf16[20,256,128]{2,1,0:T(8,128)(2,1)S(1)}, u32[]{:S(2)}, u32[]{:S(2)}) collective-permute-start(bf16[20,256,128]{2,1,0:T(8,128)(2,1)S(1)} %copy-done), channel_id=1, source_target_pairs={{0,64},{64,0},{128,192},{192,128},{256,320},{320,256},{384,448},{4... | collective-permute-start | bytes 3932168 | tf_op jit(solution)/shard_map/ppermute | solution.py:248
  50.7 1.9 %collective-permute-start = (s32[64,128]{1,0:T(8,128)S(1)}, s32[64,128]{1,0:T(8,128)S(1)}, u32[]{:S(2)}, u32[]{:S(2)}) collective-permute-start(s32[64,128]{1,0:T(8,128)S(1)} %bitcast.16), channel_id=1, source_target_pairs={{0,64},{64,0},{128,192},{192,128},{256,320},{320,256},{384,448},{4... | collective-permute-start | bytes 98312 | tf_op jit(solution)/shard_map/ppermute | solution.py:250
  52.7 1.2 %collective-permute-done.refs_1_ = s32[64,128]{1,0:T(8,128)S(1)} collective-permute-done((s32[64,128]{1,0:T(8,128)S(1)}, s32[64,128]{1,0:T(8,128)S(1)}, u32[]{:S(2)}, u32[]{:S(2)}) %collective-permute-start) | collective-permute-done | bytes 32800 | tf_op jit(solution)/shard_map/ppermute | solution.py:250
  53.8 0.0 collective-permute-done.1.refs_3_.refs_5_
  53.8 0.0 copy-done.1
  53.8 0.4 ring_0_1.1
  54.3 5.1 %collective-permute-start.7 = (bf16[128,768]{1,0:T(8,128)(2,1)S(1)}, bf16[128,768]{1,0:T(8,128)(2,1)S(1)}, u32[]{:S(2)}, u32[]{:S(2)}) collective-permute-start(bf16[128,768]{1,0:T(8,128)(2,1)S(1)} %ring_0_1.1), channel_id=1, source_target_pairs={{0,128},{64,960},{128,256},{192,64},{256,384},{320,192},{384,512},... | collective-permute-start | bytes 589832 | tf_op jit(solution)/shard_map/ppermute | solution.py:299
  59.4 0.4 ring_0_0.1
  59.8 3.0 %collective-permute-start.2 = (bf16[128,768]{1,0:T(8,128)(2,1)S(1)}, bf16[128,768]{1,0:T(8,128)(2,1)S(1)}, u32[]{:S(2)}, u32[]{:S(2)}) collective-permute-start(bf16[128,768]{1,0:T(8,128)(2,1)S(1)} %ring_0_0.1), channel_id=1, source_target_pairs={{0,128},{64,960},{128,256},{192,64},{256,384},{320,192},{384,512},... | collective-permute-start | bytes 589832 | tf_op jit(solution)/shard_map/ppermute | solution.py:299
  62.8 0.0 collective-permute-done.7.refs_6_
  62.8 0.6 ring_1_1.1
  63.4 4.5 %collective-permute-start.8 = (bf16[2,128,768]{2,1,0:T(8,128)(2,1)S(1)}, bf16[2,128,768]{2,1,0:T(8,128)(2,1)S(1)}, u32[]{:S(2)}, u32[]{:S(2)}) collective-permute-start(bf16[2,128,768]{2,1,0:T(8,128)(2,1)S(1)} %ring_1_1.1), channel_id=1, source_target_pairs={{0,128},{64,960},{128,256},{192,64},{256,384},{320,192},{384,512},... | collective-permute-start | bytes 1179656 | tf_op jit(solution)/shard_map/ppermute | solution.py:299
  67.9 0.0 collective-permute-done.2.refs_6_
  67.9 0.6 ring_1_0.1
  68.5 2.9 %collective-permute-start.3 = (bf16[2,128,768]{2,1,0:T(8,128)(2,1)S(1)}, bf16[2,128,768]{2,1,0:T(8,128)(2,1)S(1)}, u32[]{:S(2)}, u32[]{:S(2)}) collective-permute-start(bf16[2,128,768]{2,1,0:T(8,128)(2,1)S(1)} %ring_1_0.1), channel_id=1, source_target_pairs={{0,128},{64,960},{128,256},{192,64},{256,384},{320,192},{384,512},... | collective-permute-start | bytes 1179656 | tf_op jit(solution)/shard_map/ppermute | solution.py:299
  71.3 1.3 %collective-permute-done.8.refs_6_ = bf16[2,128,768]{2,1,0:T(8,128)(2,1)S(1)} collective-permute-done((bf16[2,128,768]{2,1,0:T(8,128)(2,1)S(1)}, bf16[2,128,768]{2,1,0:T(8,128)(2,1)S(1)}, u32[]{:S(2)}, u32[]{:S(2)}) %collective-permute-start.8) | collective-permute-done | bytes 393248 | tf_op jit(solution)/shard_map/ppermute | solution.py:299
  72.6 0.6 ring_2_1.1
  73.1 5.3 %collective-permute-start.9 = (bf16[2,128,768]{2,1,0:T(8,128)(2,1)S(1)}, bf16[2,128,768]{2,1,0:T(8,128)(2,1)S(1)}, u32[]{:S(2)}, u32[]{:S(2)}) collective-permute-start(bf16[2,128,768]{2,1,0:T(8,128)(2,1)S(1)} %ring_2_1.1), channel_id=1, source_target_pairs={{0,128},{64,960},{128,256},{192,64},{256,384},{320,192},{384,512},... | collective-permute-start | bytes 1179656 | tf_op jit(solution)/shard_map/ppermute | solution.py:299
  78.5 0.0 collective-permute-done.3.refs_6_
  78.5 0.6 ring_2_0.1
  79.1 3.6 %collective-permute-start.4 = (bf16[2,128,768]{2,1,0:T(8,128)(2,1)S(1)}, bf16[2,128,768]{2,1,0:T(8,128)(2,1)S(1)}, u32[]{:S(2)}, u32[]{:S(2)}) collective-permute-start(bf16[2,128,768]{2,1,0:T(8,128)(2,1)S(1)} %ring_2_0.1), channel_id=1, source_target_pairs={{0,128},{64,960},{128,256},{192,64},{256,384},{320,192},{384,512},... | collective-permute-start | bytes 1179656 | tf_op jit(solution)/shard_map/ppermute | solution.py:299
  82.7 0.5 collective-permute-done.9.refs_6_
  83.2 0.6 ring_3_1.1
  83.8 5.3 %collective-permute-start.10 = (bf16[128,768]{1,0:T(8,128)(2,1)S(1)}, bf16[128,768]{1,0:T(8,128)(2,1)S(1)}, u32[]{:S(2)}, u32[]{:S(2)}) collective-permute-start(bf16[128,768]{1,0:T(8,128)(2,1)S(1)} %get-tuple-element.18), channel_id=1, source_target_pairs={{0,128},{64,960},{128,256},{192,64},{256,384},{320,192},{384,512},... | collective-permute-start | bytes 589832 | tf_op jit(solution)/shard_map/ppermute | solution.py:299
  89.1 0.0 copy-start.2
  89.1 0.0 copy-start.3
  89.1 4.5 %collective-permute-start.11 = (bf16[128,768]{1,0:T(8,128)(2,1)S(1)}, bf16[128,768]{1,0:T(8,128)(2,1)S(1)}, u32[]{:S(2)}, u32[]{:S(2)}) collective-permute-start(bf16[128,768]{1,0:T(8,128)(2,1)S(1)} %get-tuple-element.19), channel_id=1, source_target_pairs={{0,192},{64,896},{128,320},{192,0},{256,448},{320,128},{384,576},{... | collective-permute-start | bytes 589832 | tf_op jit(solution)/shard_map/ppermute | solution.py:299
  93.7 0.0 collective-permute-done.4.refs_6_
  93.7 0.6 ring_3_0.1
  94.3 1.9 %collective-permute-start.5 = (bf16[128,768]{1,0:T(8,128)(2,1)S(1)}, bf16[128,768]{1,0:T(8,128)(2,1)S(1)}, u32[]{:S(2)}, u32[]{:S(2)}) collective-permute-start(bf16[128,768]{1,0:T(8,128)(2,1)S(1)} %get-tuple-element.16), channel_id=1, source_target_pairs={{0,128},{64,960},{128,256},{192,64},{256,384},{320,192},{384,512},... | collective-permute-start | bytes 589832 | tf_op jit(solution)/shard_map/ppermute | solution.py:299
  96.2 2.2 %collective-permute-start.6 = (bf16[128,768]{1,0:T(8,128)(2,1)S(1)}, bf16[128,768]{1,0:T(8,128)(2,1)S(1)}, u32[]{:S(2)}, u32[]{:S(2)}) collective-permute-start(bf16[128,768]{1,0:T(8,128)(2,1)S(1)} %get-tuple-element.17), channel_id=1, source_target_pairs={{0,192},{64,896},{128,320},{192,0},{256,448},{320,128},{384,576},{... | collective-permute-start | bytes 589832 | tf_op jit(solution)/shard_map/ppermute | solution.py:299
  98.5 0.0 copy-done.2
  98.5 0.0 copy-done.3
  98.5 0.4 spread.1.spread_ref
  98.9 0.6 own.1.own_ref
  99.4 0.0 collective-permute-done.10.refs_2_
  99.4 0.0 collective-permute-done.11.refs_3_
  99.4 1.5 %collective-permute-done.5.refs_0_ = bf16[128,768]{1,0:T(8,128)(2,1)S(1)} collective-permute-done((bf16[128,768]{1,0:T(8,128)(2,1)S(1)}, bf16[128,768]{1,0:T(8,128)(2,1)S(1)}, u32[]{:S(2)}, u32[]{:S(2)}) %collective-permute-start.5) | collective-permute-done | bytes 196640 | tf_op jit(solution)/shard_map/ppermute | solution.py:299
  101.0 3.4 %collective-permute-done.6.refs_1_ = bf16[128,768]{1,0:T(8,128)(2,1)S(1)} collective-permute-done((bf16[128,768]{1,0:T(8,128)(2,1)S(1)}, bf16[128,768]{1,0:T(8,128)(2,1)S(1)}, u32[]{:S(2)}, u32[]{:S(2)}) %collective-permute-start.6) | collective-permute-done | bytes 196640 | tf_op jit(solution)/shard_map/ppermute | solution.py:299
  104.4 1.2 %ring_last.1 = f32[128,1,1536]{2,1,0:T(1,128)} custom-call(f32[128,1536]{1,0:T(8,128)S(1)} %own.1.own_ref, bf16[128,768]{1,0:T(8,128)(2,1)S(1)} %collective-permute-done.5.refs_0_, bf16[128,768]{1,0:T(8,128)(2,1)S(1)} %collective-permute-done.6.refs_1_, bf16[128,768]{1,0:T(8,128)(2,1)S(1)} %collective-permute-done.10.refs_2_, ...), custom_call_target="tpu_custom_call" | custom-call | flops 589824 | bytes 2359296 | tf_op jit(solution)/shard_map/ring_last/pallas_call | solution.py:300
  105.6 0.0 all-to-all-done
  105.6 1.1 %combine.1 = bf16[16,2048]{1,0:T(8,128)(2,1)} custom-call(bf16[2,32,512]{2,1,0:T(8,128)(2,1)S(1)} %spread.1.spread_ref, bf16[512,1024]{1,0:T(8,128)(2,1)S(1)} %bitcast.15), custom_call_target="tpu_custom_call" | custom-call | flops 134217728 | bytes 1048576 | tf_op jit(solution)/shard_map/combine/pallas_call | solution.py:313
  (2 shorter events, 0.0 us)
Async XLA Ops:
  2.1 36.0 %all-to-all-start.1 = ((s32[64,1,128]{2,1,0:T(1,128)}), s32[64,1,128]{2,1,0:T(1,128)S(1)}, u32[]{:S(2)}, u32[]{:S(2)}) async-start(s32[64,1,128]{2,1,0:T(1,128)} %get-tuple-element.13), calls=%async_computation.1 | async-start | bytes 65536 | tf_op jit(solution)/shard_map/all_to_all | solution.py:204
  32.6 14.7 %copy-start = (bf16[20,256,128]{2,1,0:T(8,128)(2,1)S(1)}, bf16[20,256,128]{2,1,0:T(8,128)(2,1)}, u32[]{:S(2)}) copy-start(bf16[20,256,128]{2,1,0:T(8,128)(2,1)} %get-tuple-element.15.refs_4_) | copy-start | bytes 3932164
  32.6 21.3 %copy-start.1 = (bf16[8,256,128]{2,1,0:T(8,128)(2,1)S(1)}, bf16[8,256,128]{2,1,0:T(8,128)(2,1)}, u32[]{:S(2)}) copy-start(bf16[8,256,128]{2,1,0:T(8,128)(2,1)} %get-tuple-element.14.refs_2_) | copy-start | bytes 1572868
  38.2 67.4 %all-to-all-start = ((bf16[64,8,1024]{2,1,0:T(8,128)(2,1)}), bf16[64,8,1024]{2,1,0:T(8,128)(2,1)S(1)}, u32[]{:S(2)}, u32[]{:S(2)}) async-start(bf16[64,8,1024]{2,1,0:T(8,128)(2,1)} %bitcast.30), calls=%async_computation | async-start | bytes 2097152 | tf_op jit(solution)/shard_map/all_to_all | solution.py:238
  47.3 6.5 %collective-permute-start.1 = (bf16[20,256,128]{2,1,0:T(8,128)(2,1)S(1)}, bf16[20,256,128]{2,1,0:T(8,128)(2,1)S(1)}, u32[]{:S(2)}, u32[]{:S(2)}) collective-permute-start(bf16[20,256,128]{2,1,0:T(8,128)(2,1)S(1)} %copy-done), channel_id=1, source_target_pairs={{0,64},{64,0},{128,192},{192,128},{256,320},{320,256},{384,448},{4... | collective-permute-start | bytes 3932168 | tf_op jit(solution)/shard_map/ppermute | solution.py:248
  50.7 3.1 %collective-permute-start = (s32[64,128]{1,0:T(8,128)S(1)}, s32[64,128]{1,0:T(8,128)S(1)}, u32[]{:S(2)}, u32[]{:S(2)}) collective-permute-start(s32[64,128]{1,0:T(8,128)S(1)} %bitcast.16), channel_id=1, source_target_pairs={{0,64},{64,0},{128,192},{192,128},{256,320},{320,256},{384,448},{4... | collective-permute-start | bytes 98312 | tf_op jit(solution)/shard_map/ppermute | solution.py:250
  54.3 8.5 %collective-permute-start.7 = (bf16[128,768]{1,0:T(8,128)(2,1)S(1)}, bf16[128,768]{1,0:T(8,128)(2,1)S(1)}, u32[]{:S(2)}, u32[]{:S(2)}) collective-permute-start(bf16[128,768]{1,0:T(8,128)(2,1)S(1)} %ring_0_1.1), channel_id=1, source_target_pairs={{0,128},{64,960},{128,256},{192,64},{256,384},{320,192},{384,512},... | collective-permute-start | bytes 589832 | tf_op jit(solution)/shard_map/ppermute | solution.py:299
  59.8 8.0 %collective-permute-start.2 = (bf16[128,768]{1,0:T(8,128)(2,1)S(1)}, bf16[128,768]{1,0:T(8,128)(2,1)S(1)}, u32[]{:S(2)}, u32[]{:S(2)}) collective-permute-start(bf16[128,768]{1,0:T(8,128)(2,1)S(1)} %ring_0_0.1), channel_id=1, source_target_pairs={{0,128},{64,960},{128,256},{192,64},{256,384},{320,192},{384,512},... | collective-permute-start | bytes 589832 | tf_op jit(solution)/shard_map/ppermute | solution.py:299
  63.4 9.2 %collective-permute-start.8 = (bf16[2,128,768]{2,1,0:T(8,128)(2,1)S(1)}, bf16[2,128,768]{2,1,0:T(8,128)(2,1)S(1)}, u32[]{:S(2)}, u32[]{:S(2)}) collective-permute-start(bf16[2,128,768]{2,1,0:T(8,128)(2,1)S(1)} %ring_1_1.1), channel_id=1, source_target_pairs={{0,128},{64,960},{128,256},{192,64},{256,384},{320,192},{384,512},... | collective-permute-start | bytes 1179656 | tf_op jit(solution)/shard_map/ppermute | solution.py:299
  68.5 10.0 %collective-permute-start.3 = (bf16[2,128,768]{2,1,0:T(8,128)(2,1)S(1)}, bf16[2,128,768]{2,1,0:T(8,128)(2,1)S(1)}, u32[]{:S(2)}, u32[]{:S(2)}) collective-permute-start(bf16[2,128,768]{2,1,0:T(8,128)(2,1)S(1)} %ring_1_0.1), channel_id=1, source_target_pairs={{0,128},{64,960},{128,256},{192,64},{256,384},{320,192},{384,512},... | collective-permute-start | bytes 1179656 | tf_op jit(solution)/shard_map/ppermute | solution.py:299
  73.1 10.0 %collective-permute-start.9 = (bf16[2,128,768]{2,1,0:T(8,128)(2,1)S(1)}, bf16[2,128,768]{2,1,0:T(8,128)(2,1)S(1)}, u32[]{:S(2)}, u32[]{:S(2)}) collective-permute-start(bf16[2,128,768]{2,1,0:T(8,128)(2,1)S(1)} %ring_2_1.1), channel_id=1, source_target_pairs={{0,128},{64,960},{128,256},{192,64},{256,384},{320,192},{384,512},... | collective-permute-start | bytes 1179656 | tf_op jit(solution)/shard_map/ppermute | solution.py:299
  79.1 14.6 %collective-permute-start.4 = (bf16[2,128,768]{2,1,0:T(8,128)(2,1)S(1)}, bf16[2,128,768]{2,1,0:T(8,128)(2,1)S(1)}, u32[]{:S(2)}, u32[]{:S(2)}) collective-permute-start(bf16[2,128,768]{2,1,0:T(8,128)(2,1)S(1)} %ring_2_0.1), channel_id=1, source_target_pairs={{0,128},{64,960},{128,256},{192,64},{256,384},{320,192},{384,512},... | collective-permute-start | bytes 1179656 | tf_op jit(solution)/shard_map/ppermute | solution.py:299
  83.8 15.7 %collective-permute-start.10 = (bf16[128,768]{1,0:T(8,128)(2,1)S(1)}, bf16[128,768]{1,0:T(8,128)(2,1)S(1)}, u32[]{:S(2)}, u32[]{:S(2)}) collective-permute-start(bf16[128,768]{1,0:T(8,128)(2,1)S(1)} %get-tuple-element.18), channel_id=1, source_target_pairs={{0,128},{64,960},{128,256},{192,64},{256,384},{320,192},{384,512},... | collective-permute-start | bytes 589832 | tf_op jit(solution)/shard_map/ppermute | solution.py:299
  89.1 9.4 %copy-start.2 = (f32[1,16,8]{1,2,0:T(8,128)S(1)}, f32[1,16,8]{1,2,0:T(8,128)}, u32[]{:S(2)}) copy-start(f32[1,16,8]{1,2,0:T(8,128)} %param.7) | copy-start | bytes 1540
  89.1 9.4 %copy-start.3 = (s32[1,128]{1,0:T(1,128)S(1)}, s32[1,128]{1,0:T(1,128)}, u32[]{:S(2)}) copy-start(s32[1,128]{1,0:T(1,128)} %get-tuple-element.11.tgt_ref) | copy-start | bytes 1540
  89.1 10.3 %collective-permute-start.11 = (bf16[128,768]{1,0:T(8,128)(2,1)S(1)}, bf16[128,768]{1,0:T(8,128)(2,1)S(1)}, u32[]{:S(2)}, u32[]{:S(2)}) collective-permute-start(bf16[128,768]{1,0:T(8,128)(2,1)S(1)} %get-tuple-element.19), channel_id=1, source_target_pairs={{0,192},{64,896},{128,320},{192,0},{256,448},{320,128},{384,576},{... | collective-permute-start | bytes 589832 | tf_op jit(solution)/shard_map/ppermute | solution.py:299
  94.3 6.7 %collective-permute-start.5 = (bf16[128,768]{1,0:T(8,128)(2,1)S(1)}, bf16[128,768]{1,0:T(8,128)(2,1)S(1)}, u32[]{:S(2)}, u32[]{:S(2)}) collective-permute-start(bf16[128,768]{1,0:T(8,128)(2,1)S(1)} %get-tuple-element.16), channel_id=1, source_target_pairs={{0,128},{64,960},{128,256},{192,64},{256,384},{320,192},{384,512},... | collective-permute-start | bytes 589832 | tf_op jit(solution)/shard_map/ppermute | solution.py:299
  96.2 8.2 %collective-permute-start.6 = (bf16[128,768]{1,0:T(8,128)(2,1)S(1)}, bf16[128,768]{1,0:T(8,128)(2,1)S(1)}, u32[]{:S(2)}, u32[]{:S(2)}) collective-permute-start(bf16[128,768]{1,0:T(8,128)(2,1)S(1)} %get-tuple-element.17), channel_id=1, source_target_pairs={{0,192},{64,896},{128,320},{192,0},{256,448},{320,128},{384,576},{... | collective-permute-start | bytes 589832 | tf_op jit(solution)/shard_map/ppermute | solution.py:299
